TPU v7x, 32 devices: a whole 2x2x4 slice. The times are simulated.
32 devices in a mesh: groups: 2 (over y), seq: 4 (over z), tp: 4 (over x, core).
Axes of the slice: x: 2, y: 2, z: 4, core: 2. Of those that a mesh axis runs over, the one named last changes fastest.
Arguments:
- query: bfloat16 [4096, 2048], P(('groups', 'seq'), 'tp'), parts along dimension 0, may hold values from -64 to 64
- key_head_rows: bfloat16 [4096, 512], P(('groups', 'seq'), 'tp'), parts along dimension 0, may hold values from -64 to 64
- value_head_rows: bfloat16 [4096, 512], P(('groups', 'seq'), 'tp'), parts along dimension 0, may hold values from -6 to 6
- output_gradient: bfloat16 [4096, 2048], P(('groups', 'seq'), 'tp'), parts along dimension 0, may hold values from -16 to 16
- doc_blocks: int32 [32, 8], P(('groups', 'seq')), parts along dimension 0, may hold values from 0 to 13, as said below
- w_query: bfloat16 [4096, 2048], P(None, 'tp'), may hold values from -0.5 to 0.5
- key_weight: bfloat16 [4096, 512], P(None, 'tp'), may hold values from -0.5 to 0.5
- value_weight: bfloat16 [4096, 512], P(None, 'tp'), may hold values from -0.5 to 0.5
Outputs:
- input_grad: bfloat16 [4096, 4096], P(('groups', 'seq'), 'tp'), parts along dimension 0
There are 2 independent parts, one for each index of `groups`. A program takes and returns all parts, laid end to end along the dimension named above; an argument that names none is the same for every part. Nothing has to cross between parts.
Inputs may be any that keep to these rules, and one draw needn't show every extreme that they name: `doc_blocks`: row b holds max(b - o, 0) for 8 distinct offsets o of 2 to 12; every row b that starts a shard of 512 positions uses the offset 12, and the last row uses the offset 2.
All inputs are finite; a program needn't handle non-finite values.
Results may differ from a plain program's by a relative error of at most 0.014.
Values may be sent and summed in bfloat16 or wider, within the bound.
A program may use at most 128 MiB of HBM per device.

v0:
```python
import functools
import math

import jax
import jax.numpy as jnp
from jax import lax
from jax.experimental import pallas as pl
from jax.experimental.pallas import tpu as pltpu
from jax.sharding import PartitionSpec as P

HEAD_WIDTH = 128
BLOCK_POSITIONS = 128
MESH_ID = pl.DeviceIdType.MESH


def dot_t(a, b):
    return lax.dot_general(a, b, (((1,), (1,)), ((), ())), preferred_element_type=jnp.float32)


def dot_n(a, b):
    return lax.dot_general(a, b, (((1,), (0,)), ((), ())), preferred_element_type=jnp.float32)


def dot_lt(a, b):
    return lax.dot_general(a, b, (((0,), (0,)), ((), ())), preferred_element_type=jnp.float32)


def attention_kernel(
    shards,
    reach,
    places,
    q_ref,
    k_ref,
    v_ref,
    g_ref,
    docs_ref,
    wq_hbm,
    wk_hbm,
    wv_hbm,
    out_ref,
    dq_ref,
    dkv_ref,
    dkv_now,
    dkv_all,
    wk_all,
    wv_all,
    wq_ref,
    wk_ref,
    wv_ref,
    near_sum,
    pair_out,
    pair_in,
    far_out,
    far_in,
    weight_sem,
    pair_send,
    pair_recv,
    far_send,
    far_recv,
    fetch_send,
    fetch_recv,
    gather_send,
    gather_recv,
    kv_win,
    q_heads,
    g_heads,
    stats,
    dq_sum,
    probs,
    kv_sum,
    ret_out,
    ret_in,
    send_sem,
    recv_sem,
    ret_send,
    ret_recv,
):
    B = BLOCK_POSITIONS
    rows = k_ref.shape[0]
    nb = rows // B
    heads = q_ref.shape[1] // HEAD_WIDTH
    listed_count = docs_ref.shape[1]
    me = lax.axis_index("seq")
    scale = HEAD_WIDTH ** -0.5
    scale2 = scale * math.log2(math.e)
    has_next = me + 1 < shards
    has_prev = me >= 1

    pairs = places // 2
    place = lax.axis_index("tp")
    my_pair = place // 2
    parity = place % 2
    partner = my_pair * 2 + 1 - parity
    cols = out_ref.shape[1]

    def peer_of(k):
        return lax.rem(my_pair + k, pairs) * 2 + parity

    def owner_of(k, mine):
        return lax.rem(my_pair + k, pairs) * 2 + (parity if mine else 1 - parity)

    barrier = pltpu.get_barrier_semaphore()
    others = [(k, m) for k in range(pairs) for m in range(2) if (k, m) != (0, 0)]
    for k, m in others:
        pl.semaphore_signal(barrier, inc=1, device_id={"tp": owner_of(k, m == 0)}, device_id_type=MESH_ID)

    @pl.when(has_next)
    def _():
        pl.semaphore_signal(barrier, inc=1, device_id={"seq": me + 1}, device_id_type=MESH_ID)

    @pl.when(has_prev)
    def _():
        pl.semaphore_signal(barrier, inc=1, device_id={"seq": me - 1}, device_id_type=MESH_ID)

    pl.semaphore_wait(barrier, has_next.astype(jnp.int32) + has_prev.astype(jnp.int32) + places - 1)

    whole = [
        pltpu.make_async_copy(wq_hbm, wq_ref, weight_sem.at[0]),
        pltpu.make_async_copy(wk_hbm, wk_ref, weight_sem.at[1]),
        pltpu.make_async_copy(wv_hbm, wv_ref, weight_sem.at[2]),
    ]
    for copy in whole:
        copy.start()

    def forward(d, c):
        src = (k_ref, v_ref)[c] if d == 0 else kv_win.at[d - 1, c]
        return pltpu.make_async_remote_copy(
            src_ref=src,
            dst_ref=kv_win.at[d, c],
            send_sem=send_sem.at[d, c],
            recv_sem=recv_sem.at[d, c],
            device_id={"seq": jnp.minimum(me + 1, shards - 1)},
            device_id_type=MESH_ID,
        )

    def backward(d, c):
        return pltpu.make_async_remote_copy(
            src_ref=ret_out.at[d - 1, c],
            dst_ref=ret_in.at[d - 1, c],
            send_sem=ret_send.at[d - 1, c],
            recv_sem=ret_recv.at[d - 1, c],
            device_id={"seq": jnp.maximum(me - 1, 0)},
            device_id_type=MESH_ID,
        )

    @pl.when(has_next)
    def _():
        forward(0, 0).start()

    for i in range(nb):
        for h in range(heads):
            q_heads[i, h * B : (h + 1) * B, :] = q_ref[i * B : (i + 1) * B, h * HEAD_WIDTH : (h + 1) * HEAD_WIDTH]
            g_heads[i, h * B : (h + 1) * B, :] = g_ref[i * B : (i + 1) * B, h * HEAD_WIDTH : (h + 1) * HEAD_WIDTH]
    width = heads * B
    key_row = lax.broadcasted_iota(jnp.int32, (B, width), 0)
    query_row = lax.broadcasted_iota(jnp.int32, (B, width), 1) & (B - 1)
    own_mask = key_row <= query_row

    def span_of(owner):
        return pl.ds(pl.multiple_of(owner * cols, cols), cols)

    def fetch(k, m, c):
        owner = owner_of(k, m == 0)
        return pltpu.make_async_remote_copy(
            src_ref=(wk_hbm, wv_hbm)[c].at[span_of(owner)],
            dst_ref=(wk_all, wv_all)[c].at[k, m],
            send_sem=fetch_send.at[k, m, c],
            recv_sem=fetch_recv.at[k, m, c],
            device_id={"tp": owner},
            device_id_type=MESH_ID,
        )

    def gather(k, m):
        return pltpu.make_async_remote_copy(
            src_ref=dkv_all.at[k, 0] if m == 1 and k > 0 else dkv_ref,
            dst_ref=dkv_all.at[k, m],
            send_sem=gather_send.at[k, m],
            recv_sem=gather_recv.at[k, m],
            device_id={"tp": partner if m == 1 else peer_of(k)},
            device_id_type=MESH_ID,
        )

    @pl.when(has_next)
    def _():
        for k, m in others:
            for c in range(2):
                fetch(k, m, c).start()

    def keys_of(d):
        return (k_ref, v_ref) if d == 0 else (kv_win.at[d - 1, 0], kv_win.at[d - 1, 1])

    def key_span(d, i):
        if isinstance(i, int) and d == 0:
            return 0, i + 1
        if isinstance(i, int) and d == reach:
            return i, nb
        return 0, nb

    def biased(d, i, j, raw):
        offset = d * nb + i - j
        if isinstance(i, int) and offset == 0:
            return jnp.where(own_mask, raw, -jnp.inf), jnp.float32(0.0)
        if isinstance(i, int) and offset == 1:
            return jnp.where(own_mask, -jnp.inf, raw), jnp.float32(0.0)
        key_block = (me - d) * nb + j
        hits = jnp.int32(0)
        for n in range(listed_count):
            hits = hits | (docs_ref[i, n] == key_block).astype(jnp.int32)
        ok = (hits > 0) & (offset >= 2)
        return raw, jnp.where(ok, jnp.float32(0.0), jnp.float32(-jnp.inf))

    def raw_blocks(d, i):
        low, high = key_span(d, i)
        raw = dot_t(keys_of(d)[0][low * B : high * B, :], q_heads[i])
        return [
            biased(d, i, j, raw[(j - low) * B : (j - low + 1) * B]) for j in range(low, high)
        ]

    def stats_step(d, i, fresh):
        blocks = raw_blocks(d, i)
        tops = [jnp.max(raw, axis=0, keepdims=True) * scale2 + bias for raw, bias in blocks]
        new = functools.reduce(jnp.maximum, tops)
        if d > 0:
            old = stats[i, 0:1, :]
            new = jnp.maximum(old, new)
        total = 0.0
        for raw, bias in blocks:
            total = total + jnp.sum(jnp.exp2(raw * scale2 + (bias - new)), axis=0, keepdims=True)
        if d > 0:
            total = total + stats[i, 1:2, :] * jnp.exp2(old - new)
        stats[i, 0:1, :] = new
        stats[i, 1:2, :] = total

    def value_step(d, i, fresh):
        low, high = key_span(d, i)
        top = stats[i, 0:1, :]
        inverse = stats[i, 1:2, :]
        parts = [
            (jnp.exp2(raw * scale2 + (bias - top)) * inverse).astype(jnp.bfloat16)
            for raw, bias in raw_blocks(d, i)
        ]
        prob_half = jnp.concatenate(parts, axis=0)
        probs[d, i, low * B : high * B, :] = prob_half
        term = dot_n(prob_half, g_heads[i])
        if fresh:
            kv_sum[d, 1, low * B : high * B, :] = term
        else:
            kv_sum[d, 1, low * B : high * B, :] += term

    def delta_step(d, i, fresh):
        low, high = key_span(d, i)
        prob_grad = dot_t(keys_of(d)[1][low * B : high * B, :], g_heads[i])
        prob = probs[d, i, low * B : high * B, :].astype(jnp.float32)
        stats[i, 2:3, :] += jnp.sum(prob * prob_grad, axis=0, keepdims=True)

    def grad_step(d, i, fresh):
        low, high = key_span(d, i)
        keys = keys_of(d)[0][low * B : high * B, :]
        prob_grad = dot_t(keys_of(d)[1][low * B : high * B, :], g_heads[i])
        prob = probs[d, i, low * B : high * B, :].astype(jnp.float32)
        score_half = (prob * (prob_grad - stats[i, 2:3, :])).astype(jnp.bfloat16)
        term = dot_n(score_half, q_heads[i])
        if fresh:
            kv_sum[d, 0, low * B : high * B, :] = term
        else:
            kv_sum[d, 0, low * B : high * B, :] += term
        dq_sum[i] += dot_lt(keys, score_half)

    def over_blocks(d, step):
        if d == 0:
            for i in range(nb - 1, -1, -1):
                step(d, i, i == nb - 1)
            return
        step(d, 0, True)
        if d == reach:
            for i in range(1, nb):
                step(d, i, False)
            return

        def one(i, carry):
            step(d, i, False)
            return carry

        lax.fori_loop(1, nb, one, 0)

    def present(d, step):
        @pl.when(me >= d)
        def _():
            over_blocks(d, step)

    def arrive(d, c):
        @pl.when(me >= d)
        def _():
            forward(d - 1, c).wait_recv()

        if d < reach:

            @pl.when((me >= d) & has_next)
            def _():
                forward(d, c).start()

    def start_values():
        @pl.when(has_next)
        def _():
            forward(0, 1).start()

    def scaled(d, c):
        return kv_sum[d, c] * scale if c == 0 else kv_sum[d, c]

    def send_first(d, c):
        first = me >= d if d == reach else (me >= d) & jnp.logical_not(has_next)

        @pl.when(first)
        def _():
            ret_out[d - 1, c] = scaled(d, c).astype(jnp.bfloat16)
            backward(d, c).start()

    def send_on(d, c):
        @pl.when((me >= d) & has_next)
        def _():
            backward(d + 1, c).wait_recv()
            ret_out[d - 1, c] = (scaled(d, c) + ret_in[d, c].astype(jnp.float32)).astype(jnp.bfloat16)
            backward(d, c).start()

    for d in range(reach + 1):
        if d > 0:
            arrive(d, 0)
        if d == reach - 1:
            start_values()
        present(d, stats_step)

    for i in range(nb):
        stats[i, 1:2, :] = 1.0 / stats[i, 1:2, :]
        stats[i, 2:3, :] = jnp.zeros((1, width), jnp.float32)
        dq_sum[i] = jnp.zeros((HEAD_WIDTH, width), jnp.float32)

    for n in range(1, reach):
        present(reach - n + 1, value_step)
        send_first(reach - n + 1, 1)
        arrive(n, 1)
    present(1, value_step)
    send_first(1, 1)
    present(0, value_step)
    for d in range(reach):
        present(d, delta_step)
    arrive(reach, 1)
    present(reach, delta_step)

    for d in range(reach, -1, -1):
        if d >= 2:
            send_on(d - 1, 1)
        present(d, grad_step)
        if d >= 1:
            send_first(d, 0)

    for i in range(nb):
        turned = (dq_sum[i] * scale).T.astype(jnp.bfloat16)
        for h in range(heads):
            dq_ref[i * B : (i + 1) * B, h * HEAD_WIDTH : (h + 1) * HEAD_WIDTH] = turned[h * B : (h + 1) * B]

    for c in range(2):
        dkv_now[:, c * HEAD_WIDTH : (c + 1) * HEAD_WIDTH] = jnp.where(
            has_next, jnp.float32(0.0), scaled(0, c)
        ).astype(jnp.bfloat16)

    chunks = nb
    step_rows = rows // chunks
    for copy in whole:
        copy.wait()

    def term(owner, c):
        span = pl.ds(pl.multiple_of(owner * cols, cols), cols)
        part = slice(c * step_rows, (c + 1) * step_rows)
        value = dot_t(dq_ref[part, :], wq_ref[span, :])
        value = value + dot_t(dkv_now[part, :HEAD_WIDTH], wk_ref[span, :])
        return value + dot_t(dkv_now[part, HEAD_WIDTH:], wv_ref[span, :])

    def to_pair(k, c):
        return pltpu.make_async_remote_copy(
            src_ref=pair_out.at[k, c],
            dst_ref=pair_in.at[k, c],
            send_sem=pair_send.at[k, c],
            recv_sem=pair_recv.at[k, c],
            device_id={"tp": partner},
            device_id_type=MESH_ID,
        )

    def to_far(k, c):
        return pltpu.make_async_remote_copy(
            src_ref=far_out.at[k - 1, c],
            dst_ref=far_in.at[k - 1, c],
            send_sem=far_send.at[k - 1, c],
            recv_sem=far_recv.at[k - 1, c],
            device_id={"tp": peer_of(k)},
            device_id_type=MESH_ID,
        )

    def give(k, c):
        pair_out[k, c] = term(owner_of(k, False), c).astype(jnp.bfloat16)
        to_pair(k, c).start()

    def take(k, c):
        value = term(owner_of(k, True), c)
        to_pair(k, c).wait_recv()
        value = value + pair_in[k, c].astype(jnp.float32)
        if k == 0:
            near_sum[c] = value
        else:
            far_out[k - 1, c] = value.astype(jnp.bfloat16)
            to_far(k, c).start()

    order = [(k, c) for k in list(range(1, pairs)) + [0] for c in range(chunks)]
    give(*order[0])
    for n, item in enumerate(order):
        if n + 1 < len(order):
            give(*order[n + 1])
        take(*item)
        if n + 1 == (pairs - 1) * chunks:
            for d in range(reach - 1, 0, -1):
                send_on(d, 0)
    @pl.when(has_next)
    def _():
        for c in (1, 0):
            backward(1, c).wait_recv()
            dkv_ref[:, c * HEAD_WIDTH : (c + 1) * HEAD_WIDTH] = (
                scaled(0, c) + ret_in[0, c].astype(jnp.float32)
            ).astype(jnp.bfloat16)
        gather(0, 1).start()
        for k in range(1, pairs):
            gather(k, 0).start()

    def add_terms(pairs_of):
        for c in range(chunks):
            part = slice(c * step_rows, (c + 1) * step_rows)
            value = near_sum[c]
            for grads, wk, wv in pairs_of:
                value = value + dot_t(grads[part, :HEAD_WIDTH], wk[...])
                value = value + dot_t(grads[part, HEAD_WIDTH:], wv[...])
            near_sum[c] = value

    @pl.when(has_next)
    def _():
        for k, m in others:
            for c in range(2):
                fetch(k, m, c).wait_recv()
        own = span_of(place)
        add_terms([(dkv_ref, wk_ref.at[own], wv_ref.at[own])])
        gather(0, 1).wait_recv()
        add_terms([(dkv_all.at[0, 1], wk_all.at[0, 1], wv_all.at[0, 1])])
        for k in range(1, pairs):
            gather(k, 0).wait_recv()
            gather(k, 1).start()
            add_terms([(dkv_all.at[k, 0], wk_all.at[k, 0], wv_all.at[k, 0])])
        for k in range(1, pairs):
            gather(k, 1).wait_recv()
            add_terms([(dkv_all.at[k, 1], wk_all.at[k, 1], wv_all.at[k, 1])])
        for k, m in others:
            gather(k, m).wait_send()
            for c in range(2):
                fetch(k, m, c).wait_send()

    for c in range(chunks):
        value = near_sum[c]
        for k in range(1, pairs):
            to_far(k, c).wait_recv()
            value = value + far_in[k - 1, c].astype(jnp.float32)
        out_ref[c * step_rows : (c + 1) * step_rows, :] = value.astype(jnp.bfloat16)
    for k, c in order:
        to_pair(k, c).wait_send()
        if k > 0:
            to_far(k, c).wait_send()

    for d in range(reach):

        @pl.when((me >= d) & has_next)
        def _():
            for c in range(2):
                forward(d, c).wait_send()

        @pl.when(me >= d + 1)
        def _():
            for c in range(2):
                backward(d + 1, c).wait_send()


def body(
    query,
    key_head_rows,
    value_head_rows,
    output_gradient,
    doc_blocks,
    w_query,
    key_weight,
    value_weight,
):
    shards = lax.axis_size("seq")
    places = lax.axis_size("tp")
    pairs = places // 2
    reach = min(8, shards - 1)
    rows, q_width = query.shape
    nb = rows // BLOCK_POSITIONS
    cols = w_query.shape[0] // places
    width = (q_width // HEAD_WIDTH) * BLOCK_POSITIONS
    half, full = jnp.bfloat16, jnp.float32
    vmem = pl.BlockSpec(memory_space=pltpu.VMEM)
    anywhere = pl.BlockSpec(memory_space=pl.ANY)
    dma = pltpu.SemaphoreType.DMA
    return pl.pallas_call(
        functools.partial(attention_kernel, shards, reach, places),
        out_shape=jax.ShapeDtypeStruct((rows, cols), half),
        in_specs=[vmem] * 4 + [pl.BlockSpec(memory_space=pltpu.SMEM)] + [anywhere] * 3,
        out_specs=vmem,
        scratch_shapes=[
            pltpu.VMEM((rows, q_width), half),
            pltpu.VMEM((rows, 2 * HEAD_WIDTH), half),
            pltpu.VMEM((rows, 2 * HEAD_WIDTH), half),
            pltpu.VMEM((pairs, 2, rows, 2 * HEAD_WIDTH), half),
            pltpu.VMEM((pairs, 2, cols, HEAD_WIDTH), half),
            pltpu.VMEM((pairs, 2, cols, HEAD_WIDTH), half),
            pltpu.VMEM(w_query.shape, half),
            pltpu.VMEM(key_weight.shape, half),
            pltpu.VMEM(value_weight.shape, half),
            pltpu.VMEM((nb, rows // nb, cols), full),
            pltpu.VMEM((pairs, nb, rows // nb, cols), half),
            pltpu.VMEM((pairs, nb, rows // nb, cols), half),
            pltpu.VMEM((pairs - 1, nb, rows // nb, cols), half),
            pltpu.VMEM((pairs - 1, nb, rows // nb, cols), half),
            dma((3,)),
            dma((pairs, nb)),
            dma((pairs, nb)),
            dma((pairs - 1, nb)),
            dma((pairs - 1, nb)),
            dma((pairs, 2, 2)),
            dma((pairs, 2, 2)),
            dma((pairs, 2)),
            dma((pairs, 2)),
            pltpu.VMEM((reach, 2, rows, HEAD_WIDTH), half),
            pltpu.VMEM((nb, width, HEAD_WIDTH), half),
            pltpu.VMEM((nb, width, HEAD_WIDTH), half),
            pltpu.VMEM((nb, 8, width), full),
            pltpu.VMEM((nb, HEAD_WIDTH, width), full),
            pltpu.VMEM((reach + 1, nb, rows, width), half),
            pltpu.VMEM((reach + 1, 2, rows, HEAD_WIDTH), full),
            pltpu.VMEM((reach, 2, rows, HEAD_WIDTH), half),
            pltpu.VMEM((reach, 2, rows, HEAD_WIDTH), half),
            dma((reach, 2)),
            dma((reach, 2)),
            dma((reach, 2)),
            dma((reach, 2)),
        ],
        compiler_params=pltpu.CompilerParams(
            collective_id=0, has_side_effects=True, vmem_limit_bytes=60 * 1024 * 1024
        ),
        name="attention",
    )(
        query,
        key_head_rows,
        value_head_rows,
        output_gradient,
        doc_blocks,
        w_query,
        key_weight,
        value_weight,
    )


def solution(mesh):
    in_specs = (
        P(("groups", "seq"), "tp"),
        P(("groups", "seq"), "tp"),
        P(("groups", "seq"), "tp"),
        P(("groups", "seq"), "tp"),
        P(("groups", "seq"), None),
        P(None, "tp"),
        P(None, "tp"),
        P(None, "tp"),
    )
    out_specs = P(("groups", "seq"), "tp")
    return jax.shard_map(body, mesh=mesh, in_specs=in_specs, out_specs=out_specs, check_vma=False)
```

profile of v0, /device:TPU:17, one launch (start us, length us, event | category | flops | bytes accessed | tf_op | source)
XLA Modules:
  0.0 70.8 jit_solution(14360387823260814254)
XLA Ops:
  0.0 68.5 %attention.1 = bf16[512,1024]{1,0:T(8,128)(2,1)} custom-call(bf16[512,512]{1,0:T(8,128)(2,1)} %q_ref.1, bf16[512,128]{1,0:T(8,128)(2,1)} %k_ref.1, bf16[512,128]{1,0:T(8,128)(2,1)} %v_ref.1, bf16[512,512]{1,0:T(8,128)(2,1)} %g_ref.1, s32[4,8]{1,0:T(4,128)} %docs_ref.1, bf16[4096,512]{1,0:T(8,128)(2,1)} %wq_hbm.1, bf16[4096,128]{1,0:T(8,128)(2,1)} %wk_hbm.1, ...), custom_call_target="tpu_custom_call" | custom-call | tf_op jit(solution)/shard_map/attention/pallas_call | solution.py:508
  68.5 2.3 %copy.10 = bf16[512,1024]{1,0:T(8,128)(2,1)} copy(bf16[512,1024]{1,0:T(8,128)(2,1)} %attention.1) | data formatting | bytes 2097152
where the time goes:
time: 71.4 us; the launch traced here: 70.8 us
  Pallas kernels  68.5 us (96%)
  local copies, waits for them, and re-layouts  2.26 us (3%)
    pallas_call x1, Pallas kernels, body(): pl.pallas_call(functools.partial(attention_kernel, shards, reach, places)...  68.5 us
    unnamed x1, local copies, waits for them, and re-layouts  2.26 us

commit v1 on v0

v1 whole, which is shorter than its diff:
```python
import functools
import math

import jax
import jax.numpy as jnp
from jax import lax
from jax.experimental import pallas as pl
from jax.experimental.pallas import tpu as pltpu
from jax.sharding import PartitionSpec as P

HEAD_WIDTH = 128
BLOCK_POSITIONS = 128
MESH_ID = pl.DeviceIdType.MESH
SPARE_MIB = 12


def dot_t(a, b):
    return lax.dot_general(a, b, (((1,), (1,)), ((), ())), preferred_element_type=jnp.float32)


def dot_n(a, b):
    return lax.dot_general(a, b, (((1,), (0,)), ((), ())), preferred_element_type=jnp.float32)


def dot_lt(a, b):
    return lax.dot_general(a, b, (((0,), (0,)), ((), ())), preferred_element_type=jnp.float32)


FLOOR = -1e9


def attention_kernel(
    shards,
    reach,
    places,
    groups,
    q_hbm,
    k_hbm,
    v_hbm,
    g_hbm,
    docs_ref,
    wq_hbm,
    wk_hbm,
    wv_hbm,
    out_ref,
    q_ref,
    k_ref,
    v_ref,
    g_ref,
    dq_ref,
    dkv_ref,
    dkv_now,
    dkv_all,
    wk_all,
    wv_all,
    wq_ref,
    wk_ref,
    wv_ref,
    near_sum,
    pair_out,
    pair_in,
    far_out,
    far_in,
    load_sem,
    weight_sem,
    pair_send,
    pair_recv,
    far_send,
    far_recv,
    fetch_send,
    fetch_recv,
    relay_send,
    relay_recv,
    gather_send,
    gather_recv,
    kv_win,
    q_heads,
    g_heads,
    stats,
    delta,
    dq_sum,
    probs,
    kv_sum,
    ret_out,
    ret_in,
    send_sem,
    recv_sem,
    ret_send,
    ret_recv,
):
    B = BLOCK_POSITIONS
    rows = k_ref.shape[0]
    nb = rows // B
    heads = q_ref.shape[1] // HEAD_WIDTH
    listed_count = docs_ref.shape[1]
    me = lax.axis_index("seq")
    scale = HEAD_WIDTH ** -0.5
    scale2 = scale * math.log2(math.e)
    has_next = me + 1 < shards
    has_prev = me >= 1

    pairs = places // 2
    place = lax.axis_index("tp")
    my_pair = place // 2
    parity = place % 2
    partner = my_pair * 2 + 1 - parity
    cols = out_ref.shape[1]
    relayed = groups == 2
    group = lax.axis_index("groups")

    def peer_of(k):
        return lax.rem(my_pair + k, pairs) * 2 + parity

    def owner_of(k, mine):
        return lax.rem(my_pair + k, pairs) * 2 + (parity if mine else 1 - parity)

    loads = [
        pltpu.make_async_copy(src, dst, load_sem.at[n])
        for n, (src, dst) in enumerate(((k_hbm, k_ref), (q_hbm, q_ref), (v_hbm, v_ref), (g_hbm, g_ref)))
    ]
    for copy in loads:
        copy.start()

    barrier = pltpu.get_barrier_semaphore()
    others = [(k, m) for k in range(pairs) for m in range(2) if (k, m) != (0, 0)]
    for k, m in others:
        pl.semaphore_signal(barrier, inc=1, device_id={"tp": owner_of(k, m == 0)}, device_id_type=MESH_ID)
    if relayed:
        pl.semaphore_signal(barrier, inc=1, device_id={"groups": 1 - group}, device_id_type=MESH_ID)

    @pl.when(has_next)
    def _():
        pl.semaphore_signal(barrier, inc=1, device_id={"seq": me + 1}, device_id_type=MESH_ID)

    @pl.when(has_prev)
    def _():
        pl.semaphore_signal(barrier, inc=1, device_id={"seq": me - 1}, device_id_type=MESH_ID)

    greeted = places - 1 + (1 if relayed else 0)
    pl.semaphore_wait(barrier, has_next.astype(jnp.int32) + has_prev.astype(jnp.int32) + greeted)

    def forward(d, c):
        src = (k_hbm, v_hbm)[c] if d == 0 else kv_win.at[d - 1, c]
        return pltpu.make_async_remote_copy(
            src_ref=src,
            dst_ref=kv_win.at[d, c],
            send_sem=send_sem.at[d, c],
            recv_sem=recv_sem.at[d, c],
            device_id={"seq": jnp.minimum(me + 1, shards - 1)},
            device_id_type=MESH_ID,
        )

    def backward(d, c):
        return pltpu.make_async_remote_copy(
            src_ref=ret_out.at[d - 1, c],
            dst_ref=ret_in.at[d - 1, c],
            send_sem=ret_send.at[d - 1, c],
            recv_sem=ret_recv.at[d - 1, c],
            device_id={"seq": jnp.maximum(me - 1, 0)},
            device_id_type=MESH_ID,
        )

    def span_of(owner):
        return pl.ds(pl.multiple_of(owner * cols, cols), cols)

    def fetch(k, m, c):
        if isinstance(m, int):
            owner = owner_of(k, m == 0)
        else:
            owner = lax.rem(my_pair + k, pairs) * 2 + lax.rem(parity + m, 2)
        return pltpu.make_async_remote_copy(
            src_ref=(wk_hbm, wv_hbm)[c].at[span_of(owner)],
            dst_ref=(wk_all, wv_all)[c].at[k, m],
            send_sem=fetch_send.at[k, m, c],
            recv_sem=fetch_recv.at[k, m, c],
            device_id={"tp": owner},
            device_id_type=MESH_ID,
        )

    def relay(k, c):
        return pltpu.make_async_remote_copy(
            src_ref=(wk_all, wv_all)[c].at[k, group],
            dst_ref=(wk_all, wv_all)[c].at[k, group],
            send_sem=relay_send.at[k, c],
            recv_sem=relay_recv.at[k, c],
            device_id={"groups": 1 - group},
            device_id_type=MESH_ID,
        )

    def relay_in(k, c):
        return pltpu.make_async_remote_copy(
            src_ref=(wk_all, wv_all)[c].at[k, 1 - group],
            dst_ref=(wk_all, wv_all)[c].at[k, 1 - group],
            send_sem=relay_send.at[k, c],
            recv_sem=relay_recv.at[k, c],
            device_id={"groups": 1 - group},
            device_id_type=MESH_ID,
        )

    if relayed:
        fetches = [(0, 1, c) for c in range(2)] + [(k, group, c) for c in (1, 0) for k in range(1, pairs)]
    else:
        fetches = [(k, m, c) for k, m in others for c in range(2)]

    @pl.when(has_next)
    def _():
        forward(0, 0).start()
        forward(0, 1).start()
        for item in fetches:
            fetch(*item).start()

    whole = [
        pltpu.make_async_copy(wq_hbm, wq_ref, weight_sem.at[0]),
        pltpu.make_async_copy(wk_hbm, wk_ref, weight_sem.at[1]),
        pltpu.make_async_copy(wv_hbm, wv_ref, weight_sem.at[2]),
    ]
    for copy in whole:
        copy.start()

    width = heads * B
    for d in range(1, reach + 1):
        for i in range(nb):
            stats[d, i, 0:1, :] = jnp.full((1, width), FLOOR, jnp.float32)
            stats[d, i, 1:3, :] = jnp.zeros((2, width), jnp.float32)

    for copy in loads:
        copy.wait()
    for i in range(nb):
        for h in range(heads):
            q_heads[i, h * B : (h + 1) * B, :] = q_ref[i * B : (i + 1) * B, h * HEAD_WIDTH : (h + 1) * HEAD_WIDTH]
            g_heads[i, h * B : (h + 1) * B, :] = g_ref[i * B : (i + 1) * B, h * HEAD_WIDTH : (h + 1) * HEAD_WIDTH]
    key_row = lax.broadcasted_iota(jnp.int32, (B, width), 0)
    query_row = lax.broadcasted_iota(jnp.int32, (B, width), 1) & (B - 1)
    own_mask = key_row <= query_row

    def keys_of(d):
        if isinstance(d, int) and d == 0:
            return k_ref, v_ref
        return kv_win.at[d - 1, 0], kv_win.at[d - 1, 1]

    def key_span(d, i):
        if isinstance(i, int) and isinstance(d, int) and d == 0:
            return 0, i + 1
        if isinstance(i, int) and isinstance(d, int) and d == reach:
            return i, nb
        return 0, nb

    def biased(d, i, j, raw):
        offset = d * nb + i - j
        if isinstance(i, int) and offset == 0:
            return jnp.where(own_mask, raw, -jnp.inf), jnp.float32(0.0)
        if isinstance(i, int) and offset == 1:
            return jnp.where(own_mask, -jnp.inf, raw), jnp.float32(0.0)
        key_block = (me - d) * nb + j
        hits = jnp.int32(0)
        for n in range(listed_count):
            hits = hits | (docs_ref[i, n] == key_block).astype(jnp.int32)
        ok = (hits > 0) & (offset >= 2)
        return raw, jnp.where(ok, jnp.float32(0.0), jnp.float32(-jnp.inf))

    def raw_blocks(d, i):
        low, high = key_span(d, i)
        raw = dot_t(keys_of(d)[0][low * B : high * B, :], q_heads[i])
        return [
            biased(d, i, j, raw[(j - low) * B : (j - low + 1) * B]) for j in range(low, high)
        ]

    def score_step(d, i, fresh):
        low, high = key_span(d, i)
        blocks = raw_blocks(d, i)
        tops = [jnp.max(raw, axis=0, keepdims=True) * scale2 + bias for raw, bias in blocks]
        top = jnp.maximum(functools.reduce(jnp.maximum, tops), FLOOR)
        total = 0.0
        for j, (raw, bias) in enumerate(blocks):
            weight = jnp.exp2(raw * scale2 + (bias - top))
            total = total + jnp.sum(weight, axis=0, keepdims=True)
            probs[d, i, (low + j) * B : (low + j + 1) * B, :] = weight.astype(jnp.bfloat16)
        stats[d, i, 0:1, :] = top
        stats[d, i, 1:2, :] = total

    def delta_step(d, i, fresh):
        low, high = key_span(d, i)
        prob_grad = dot_t(keys_of(d)[1][low * B : high * B, :], g_heads[i])
        weight = probs[d, i, low * B : high * B, :].astype(jnp.float32)
        stats[d, i, 2:3, :] = jnp.sum(weight * prob_grad, axis=0, keepdims=True)

    def late_delta_step(d, i, fresh):
        delta_step(d, i, fresh)
        stats[d, i, 1:2, :] = jnp.ones((1, width), jnp.float32)

    def value_step(d, i, fresh):
        low, high = key_span(d, i)
        weight = probs[d, i, low * B : high * B, :].astype(jnp.float32)
        prob_half = (weight * stats[d, i, 1:2, :]).astype(jnp.bfloat16)
        probs[d, i, low * B : high * B, :] = prob_half
        term = dot_n(prob_half, g_heads[i])
        if fresh:
            kv_sum[d, 1, low * B : high * B, :] = term
        else:
            kv_sum[d, 1, low * B : high * B, :] += term

    def grad_step(d, i, fresh):
        low, high = key_span(d, i)
        keys = keys_of(d)[0][low * B : high * B, :]
        prob_grad = dot_t(keys_of(d)[1][low * B : high * B, :], g_heads[i])
        prob = probs[d, i, low * B : high * B, :].astype(jnp.float32)
        score_half = (prob * (prob_grad - delta[i, 0:1, :])).astype(jnp.bfloat16)
        term = dot_n(score_half, q_heads[i])
        if fresh:
            kv_sum[d, 0, low * B : high * B, :] = term
        else:
            kv_sum[d, 0, low * B : high * B, :] += term
        turned = dot_lt(keys, score_half)
        if isinstance(d, int) and d == 0:
            dq_sum[i] = turned
        else:
            dq_sum[i] += turned

    def over_blocks(d, step):
        if d == 0:
            for i in range(nb - 1, -1, -1):
                step(d, i, i == nb - 1)
            return
        step(d, 0, True)
        if d == reach:
            for i in range(1, nb):
                step(d, i, False)
            return

        def one(i, carry):
            step(d, i, False)
            return carry

        lax.fori_loop(1, nb, one, 0)

    def present(d, step, extra=None):
        @pl.when(me >= d if extra is None else (me >= d) & extra)
        def _():
            over_blocks(d, step)

    def arrive(d, c):
        @pl.when(me >= d)
        def _():
            forward(d - 1, c).wait_recv()

        if d < reach:

            @pl.when((me >= d) & has_next)
            def _():
                forward(d, c).start()

    def scaled(d, c):
        return kv_sum[d, c] * scale if c == 0 else kv_sum[d, c]

    def send_first(d, c):
        first = me >= d if d == reach else (me >= d) & jnp.logical_not(has_next)

        @pl.when(first)
        def _():
            ret_out[d - 1, c] = scaled(d, c).astype(jnp.bfloat16)
            backward(d, c).start()

    def send_on(d, c):
        @pl.when((me >= d) & has_next)
        def _():
            backward(d + 1, c).wait_recv()
            ret_out[d - 1, c] = (scaled(d, c) + ret_in[d, c].astype(jnp.float32)).astype(jnp.bfloat16)
            backward(d, c).start()

    present(0, score_step)
    present(0, delta_step)
    for d in range(1, reach + 1):
        arrive(d, 0)
        present(d, score_step)
        if d < reach:

            @pl.when(me > d)
            def _():
                forward(d - 1, 1).wait_recv()

                @pl.when(has_next)
                def _():
                    forward(d, 1).start()

                over_blocks(d, delta_step)

    for i in range(nb):
        tops = [stats[d, i, 0:1, :] for d in range(reach + 1)]
        top = functools.reduce(jnp.maximum, tops)
        parts = [jnp.exp2(t - top) for t in tops]
        total = functools.reduce(jnp.add, [parts[d] * stats[d, i, 1:2, :] for d in range(reach + 1)])
        inverse = 1.0 / total
        for d in range(reach + 1):
            stats[d, i, 1:2, :] = parts[d] * inverse

    for d in range(reach, -1, -1):
        present(d, value_step)
        if d > 0:
            send_first(d, 1)

    for d in range(1, reach + 1):

        @pl.when(me >= reach if d == reach else me == d)
        def _():
            forward(d - 1, 1).wait_recv()
            if d < reach:

                @pl.when(has_next)
                def _():
                    forward(d, 1).start()

            over_blocks(d, late_delta_step)

    for i in range(nb):
        delta[i, 0:1, :] = functools.reduce(
            jnp.add, [stats[d, i, 1:2, :] * stats[d, i, 2:3, :] for d in range(reach + 1)]
        )

    @pl.when(me >= reach)
    def _():
        kv_sum[reach, 0] = jnp.zeros((rows, HEAD_WIDTH), jnp.float32)

    def grads_of(i):
        grad_step(0, i, i == nb - 1)

        def one(d, carry):
            grad_step(d, i, i == nb - 1)
            return carry

        if reach > 1:
            lax.fori_loop(1, jnp.minimum(me, reach - 1) + 1, one, 0)

        @pl.when(me >= reach)
        def _():
            grad_step(reach, i, False)

        part = slice(i * B, (i + 1) * B)
        turned = (dq_sum[i] * scale).T.astype(jnp.bfloat16)
        for h in range(heads):
            dq_ref[part, h * HEAD_WIDTH : (h + 1) * HEAD_WIDTH] = turned[h * B : (h + 1) * B]
        for c in range(2):
            own = kv_sum[0, c, part, :] * scale if c == 0 else kv_sum[0, c, part, :]
            dkv_now[part, c * HEAD_WIDTH : (c + 1) * HEAD_WIDTH] = jnp.where(
                has_next, jnp.float32(0.0), own
            ).astype(jnp.bfloat16)

    chunks = nb
    step_rows = rows // chunks

    def term(owner, c):
        span = pl.ds(pl.multiple_of(owner * cols, cols), cols)
        part = slice(c * step_rows, (c + 1) * step_rows)
        value = dot_t(dq_ref[part, :], wq_ref[span, :])
        value = value + dot_t(dkv_now[part, :HEAD_WIDTH], wk_ref[span, :])
        return value + dot_t(dkv_now[part, HEAD_WIDTH:], wv_ref[span, :])

    def to_pair(k, c):
        return pltpu.make_async_remote_copy(
            src_ref=pair_out.at[k, c],
            dst_ref=pair_in.at[k, c],
            send_sem=pair_send.at[k, c],
            recv_sem=pair_recv.at[k, c],
            device_id={"tp": partner},
            device_id_type=MESH_ID,
        )

    def to_far(k, c):
        return pltpu.make_async_remote_copy(
            src_ref=far_out.at[k - 1, c],
            dst_ref=far_in.at[k - 1, c],
            send_sem=far_send.at[k - 1, c],
            recv_sem=far_recv.at[k - 1, c],
            device_id={"tp": peer_of(k)},
            device_id_type=MESH_ID,
        )

    def give(k, c):
        pair_out[k, c] = term(owner_of(k, False), c).astype(jnp.bfloat16)
        to_pair(k, c).start()

    def take(k, c):
        value = term(owner_of(k, True), c)
        to_pair(k, c).wait_recv()
        value = value + pair_in[k, c].astype(jnp.float32)
        if k == 0:
            near_sum[c] = value
        else:
            far_out[k - 1, c] = value.astype(jnp.bfloat16)
            to_far(k, c).start()

    def far_terms(c):
        for k in range(1, pairs):
            give(k, c)
        for k in range(1, pairs):
            take(k, c)

    grads_of(nb - 1)
    for copy in whole:
        copy.wait()
    far_terms(nb - 1)

    if relayed:

        @pl.when(has_next)
        def _():
            for c in (1, 0):
                for k in range(1, pairs):
                    fetch(k, group, c).wait_recv()
                    relay(k, c).start()

    for i in range(nb - 2, -1, -1):
        grads_of(i)
    for d in range(reach, 0, -1):
        send_first(d, 0)
    for i in range(nb - 2, -1, -1):
        far_terms(i)
    for d in range(reach - 1, 0, -1):
        send_on(d, 1)
    near = list(range(nb - 1, -1, -1))
    give(0, near[0])
    for n, c in enumerate(near):
        if n + 1 < len(near):
            give(0, near[n + 1])
        take(0, c)

    def gather(k, m, c):
        return pltpu.make_async_remote_copy(
            src_ref=dkv_all.at[k, 0, c] if m == 1 and k > 0 else dkv_ref.at[c],
            dst_ref=dkv_all.at[k, m, c],
            send_sem=gather_send.at[k, m, c],
            recv_sem=gather_recv.at[k, m, c],
            device_id={"tp": partner if m == 1 else peer_of(k)},
            device_id_type=MESH_ID,
        )

    def settle(c):
        @pl.when(has_next)
        def _():
            backward(1, c).wait_recv()
            dkv_ref[c] = (scaled(0, c) + ret_in[0, c].astype(jnp.float32)).astype(jnp.bfloat16)
            for k in range(1, pairs):
                gather(k, 0, c).start()
            gather(0, 1, c).start()

    def add_terms(pairs_of):
        for c in range(chunks):
            part = slice(c * step_rows, (c + 1) * step_rows)
            value = near_sum[c]
            for grads, w in pairs_of:
                value = value + dot_t(grads[part, :], w[...])
            near_sum[c] = value

    def near_adds(c):
        own = span_of(place)
        gather(0, 1, c).wait_recv()
        add_terms(
            [
                (dkv_ref.at[c], (wk_ref, wv_ref)[c].at[own]),
                (dkv_all.at[0, 1, c], (wk_all, wv_all)[c].at[0, 1]),
            ]
        )

    def far_adds(c):
        for k in range(1, pairs):
            gather(k, 0, c).wait_recv()
            gather(k, 1, c).start()
        for k in range(1, pairs):
            gather(k, 1, c).wait_recv()
            add_terms([(dkv_all.at[k, m, c], (wk_all, wv_all)[c].at[k, m]) for m in range(2)])

    settle(1)

    @pl.when(has_next)
    def _():
        for c in range(2):
            fetch(0, 1, c).wait_recv()
        near_adds(1)

    for d in range(reach - 1, 0, -1):
        send_on(d, 0)

    @pl.when(has_next)
    def _():
        for k in range(1, pairs):
            for c in range(2):
                if relayed:
                    relay_in(k, c).wait_recv()
                else:
                    for m in range(2):
                        fetch(k, m, c).wait_recv()
        far_adds(1)

    settle(0)

    @pl.when(has_next)
    def _():
        near_adds(0)
        far_adds(0)

    for c in near:
        value = near_sum[c]
        for k in range(1, pairs):
            to_far(k, c).wait_recv()
            value = value + far_in[k - 1, c].astype(jnp.float32)
        out_ref[c * step_rows : (c + 1) * step_rows, :] = value.astype(jnp.bfloat16)

    @pl.when(has_next)
    def _():
        for k, m in others:
            for c in range(2):
                gather(k, m, c).wait_send()
        for item in fetches:
            fetch(*item).wait_send()
        if relayed:
            for k in range(1, pairs):
                for c in range(2):
                    relay(k, c).wait_send()

    for c in near:
        for k in range(pairs):
            to_pair(k, c).wait_send()
            if k > 0:
                to_far(k, c).wait_send()

    for d in range(reach):

        @pl.when((me >= d) & has_next)
        def _():
            for c in range(2):
                forward(d, c).wait_send()

        @pl.when(me >= d + 1)
        def _():
            for c in range(2):
                backward(d + 1, c).wait_send()


def body(
    query,
    key_head_rows,
    value_head_rows,
    output_gradient,
    doc_blocks,
    w_query,
    key_weight,
    value_weight,
):
    shards = lax.axis_size("seq")
    places = lax.axis_size("tp")
    groups = lax.axis_size("groups")
    pairs = places // 2
    reach = min(8, shards - 1)
    rows, q_width = query.shape
    nb = rows // BLOCK_POSITIONS
    cols = w_query.shape[0] // places
    width = (q_width // HEAD_WIDTH) * BLOCK_POSITIONS
    half, full = jnp.bfloat16, jnp.float32
    vmem = pl.BlockSpec(memory_space=pltpu.VMEM)
    hbm = pl.BlockSpec(memory_space=pltpu.HBM)
    dma = pltpu.SemaphoreType.DMA
    buffers = [
        ((rows, q_width), half),
        ((rows, HEAD_WIDTH), half),
        ((rows, HEAD_WIDTH), half),
        ((rows, q_width), half),
        ((rows, q_width), half),
        ((2, rows, HEAD_WIDTH), half),
        ((rows, 2 * HEAD_WIDTH), half),
        ((pairs, 2, 2, rows, HEAD_WIDTH), half),
        ((pairs, 2, cols, HEAD_WIDTH), half),
        ((pairs, 2, cols, HEAD_WIDTH), half),
        (w_query.shape, half),
        (key_weight.shape, half),
        (value_weight.shape, half),
        ((nb, rows // nb, cols), full),
        ((pairs, nb, rows // nb, cols), half),
        ((pairs, nb, rows // nb, cols), half),
        ((pairs - 1, nb, rows // nb, cols), half),
        ((pairs - 1, nb, rows // nb, cols), half),
    ]
    later = [
        ((reach, 2, rows, HEAD_WIDTH), half),
        ((nb, width, HEAD_WIDTH), half),
        ((nb, width, HEAD_WIDTH), half),
        ((reach + 1, nb, 8, width), full),
        ((nb, 8, width), full),
        ((nb, HEAD_WIDTH, width), full),
        ((reach + 1, nb, rows, width), half),
        ((reach + 1, 2, rows, HEAD_WIDTH), full),
        ((reach, 2, rows, HEAD_WIDTH), half),
        ((reach, 2, rows, HEAD_WIDTH), half),
    ]
    used = sum(math.prod(shape) * jnp.dtype(kind).itemsize for shape, kind in buffers + later)
    limit = min(used + SPARE_MIB * 1024 * 1024, 60 * 1024 * 1024)
    return pl.pallas_call(
        functools.partial(attention_kernel, shards, reach, places, groups),
        out_shape=jax.ShapeDtypeStruct((rows, cols), half),
        in_specs=[hbm] * 4 + [pl.BlockSpec(memory_space=pltpu.SMEM)] + [hbm] * 3,
        out_specs=vmem,
        scratch_shapes=[pltpu.VMEM(*item) for item in buffers]
        + [
            dma((4,)),
            dma((3,)),
            dma((pairs, nb)),
            dma((pairs, nb)),
            dma((pairs - 1, nb)),
            dma((pairs - 1, nb)),
            dma((pairs, 2, 2)),
            dma((pairs, 2, 2)),
            dma((pairs, 2)),
            dma((pairs, 2)),
            dma((pairs, 2, 2)),
            dma((pairs, 2, 2)),
        ]
        + [pltpu.VMEM(*item) for item in later]
        + [
            dma((reach, 2)),
            dma((reach, 2)),
            dma((reach, 2)),
            dma((reach, 2)),
        ],
        compiler_params=pltpu.CompilerParams(
            collective_id=0, has_side_effects=True, vmem_limit_bytes=limit
        ),
        name="attention",
    )(
        pltpu.with_memory_space_constraint(query, pltpu.HBM),
        pltpu.with_memory_space_constraint(key_head_rows, pltpu.HBM),
        pltpu.with_memory_space_constraint(value_head_rows, pltpu.HBM),
        pltpu.with_memory_space_constraint(output_gradient, pltpu.HBM),
        doc_blocks,
        pltpu.with_memory_space_constraint(w_query, pltpu.HBM),
        pltpu.with_memory_space_constraint(key_weight, pltpu.HBM),
        pltpu.with_memory_space_constraint(value_weight, pltpu.HBM),
    )


def solution(mesh):
    in_specs = (
        P(("groups", "seq"), "tp"),
        P(("groups", "seq"), "tp"),
        P(("groups", "seq"), "tp"),
        P(("groups", "seq"), "tp"),
        P(("groups", "seq"), None),
        P(None, "tp"),
        P(None, "tp"),
        P(None, "tp"),
    )
    out_specs = P(("groups", "seq"), "tp")
    return jax.shard_map(body, mesh=mesh, in_specs=in_specs, out_specs=out_specs, check_vma=False)
```

time: 71.4 us -> 63.2 us (0.89)
  the two profiles are of different devices: /device:TPU:17 before, /device:TPU:1 now
where the time goes in v1:
time: 63.2 us; the launch traced here: 63 us
  Pallas kernels  61.4 us (97%)
  local copies, waits for them, and re-layouts  1.65 us (3%)
    pallas_call x1, Pallas kernels, body(): pl.pallas_call(functools.partial(attention_kernel, shards, reach, places,...  61.4 us
    unnamed x3, local copies, waits for them, and re-layouts  1.65 us

profile of v1, /device:TPU:1, one launch (start us, length us, event | category | flops | bytes accessed | tf_op | source)
XLA Modules:
  0.0 63.0 jit_solution(4069265597739736857)
XLA Ops:
  0.0 0.0 copy-start
  0.0 0.7 %copy-done = s32[4,8]{1,0:T(4,128)S(1)} copy-done((s32[4,8]{1,0:T(4,128)S(1)}, s32[4,8]{1,0:T(4,128)}, u32[]{:S(2)}) %copy-start) | copy-done | bytes 152
  0.7 61.4 %attention.1 = bf16[512,1024]{1,0:T(8,128)(2,1)S(1)} custom-call(bf16[512,512]{1,0:T(8,128)(2,1)} %q_hbm.1, bf16[512,128]{1,0:T(8,128)(2,1)} %k_hbm.1, bf16[512,128]{1,0:T(8,128)(2,1)} %v_hbm.1, bf16[512,512]{1,0:T(8,128)(2,1)} %g_hbm.1, s32[4,8]{1,0:T(4,128)S(1)} %copy-done, bf16[4096,512]{1,0:T(8,128)(2,1)} %wq_hbm.1, bf16[4096,128]{1,0:T(8,128)(2,1)} %wk_hbm.1, ...), custom_call_target="tpu_custom_call" | custom-call | tf_op jit(solution)/shard_map/attention/pallas_call | solution.py:695
  62.0 1.0 %copy.10 = bf16[512,1024]{1,0:T(8,128)(2,1)} copy(bf16[512,1024]{1,0:T(8,128)(2,1)S(1)} %attention.1) | data formatting | bytes 2097152
Async XLA Ops:
  0.0 0.7 %copy-start = (s32[4,8]{1,0:T(4,128)S(1)}, s32[4,8]{1,0:T(4,128)}, u32[]{:S(2)}) copy-start(s32[4,8]{1,0:T(4,128)} %docs_ref.1) | copy-start | bytes 388

commit v2 on v1

--- a/solution.py
+++ b/solution.py
@@ -38,21 +38,20 @@
     k_hbm,
     v_hbm,
     g_hbm,
-    docs_ref,
+    docs_hbm,
     wq_hbm,
     wk_hbm,
     wv_hbm,
     out_ref,
+    docs_ref,
     q_ref,
     k_ref,
     v_ref,
     g_ref,
     dq_ref,
-    dkv_ref,
     dkv_now,
     dkv_all,
-    wk_all,
-    wv_all,
+    kw_all,
     wq_ref,
     wk_ref,
     wv_ref,
@@ -116,7 +115,7 @@
 
     loads = [
         pltpu.make_async_copy(src, dst, load_sem.at[n])
-        for n, (src, dst) in enumerate(((k_hbm, k_ref), (q_hbm, q_ref), (v_hbm, v_ref), (g_hbm, g_ref)))
+        for n, (src, dst) in enumerate(((k_hbm, k_ref), (q_hbm, q_ref), (v_hbm, v_ref), (g_hbm, g_ref), (docs_hbm, docs_ref)))
     ]
     for copy in loads:
         copy.start()
@@ -163,6 +162,10 @@
     def span_of(owner):
         return pl.ds(pl.multiple_of(owner * cols, cols), cols)
 
+    def slot(k, m):
+        lane = (2 * k + m) * HEAD_WIDTH
+        return pl.ds(lane if isinstance(m, int) else pl.multiple_of(lane, HEAD_WIDTH), HEAD_WIDTH)
+
     def fetch(k, m, c):
         if isinstance(m, int):
             owner = owner_of(k, m == 0)
@@ -170,27 +173,23 @@
             owner = lax.rem(my_pair + k, pairs) * 2 + lax.rem(parity + m, 2)
         return pltpu.make_async_remote_copy(
             src_ref=(wk_hbm, wv_hbm)[c].at[span_of(owner)],
-            dst_ref=(wk_all, wv_all)[c].at[k, m],
+            dst_ref=kw_all.at[c, :, slot(k, m)],
             send_sem=fetch_send.at[k, m, c],
             recv_sem=fetch_recv.at[k, m, c],
             device_id={"tp": owner},
             device_id_type=MESH_ID,
         )
 
-    def relay(k, c):
+    def own_weights(c):
+        return pltpu.make_async_copy(
+            (wk_hbm, wv_hbm)[c].at[span_of(place)], kw_all.at[c, :, slot(0, 0)], fetch_recv.at[0, 0, c]
+        )
+
+    def relay(k, c, arriving=False):
+        which = 1 - group if arriving else group
         return pltpu.make_async_remote_copy(
-            src_ref=(wk_all, wv_all)[c].at[k, group],
-            dst_ref=(wk_all, wv_all)[c].at[k, group],
-            send_sem=relay_send.at[k, c],
-            recv_sem=relay_recv.at[k, c],
-            device_id={"groups": 1 - group},
-            device_id_type=MESH_ID,
-        )
-
-    def relay_in(k, c):
-        return pltpu.make_async_remote_copy(
-            src_ref=(wk_all, wv_all)[c].at[k, 1 - group],
-            dst_ref=(wk_all, wv_all)[c].at[k, 1 - group],
+            src_ref=kw_all.at[c, :, slot(k, which)],
+            dst_ref=kw_all.at[c, :, slot(k, which)],
             send_sem=relay_send.at[k, c],
             recv_sem=relay_recv.at[k, c],
             device_id={"groups": 1 - group},
@@ -208,6 +207,8 @@
         forward(0, 1).start()
         for item in fetches:
             fetch(*item).start()
+        for c in range(2):
+            own_weights(c).start()
 
     whole = [
         pltpu.make_async_copy(wq_hbm, wq_ref, weight_sem.at[0]),
@@ -222,6 +223,13 @@
         for i in range(nb):
             stats[d, i, 0:1, :] = jnp.full((1, width), FLOOR, jnp.float32)
             stats[d, i, 1:3, :] = jnp.zeros((2, width), jnp.float32)
+
+    for i in range(nb):
+        dq_sum[i] = jnp.zeros((HEAD_WIDTH, width), jnp.float32)
+
+    @pl.when(me >= reach)
+    def _():
+        kv_sum[reach, 0] = jnp.zeros((rows, HEAD_WIDTH), jnp.float32)
 
     for copy in loads:
         copy.wait()
@@ -285,8 +293,13 @@
         stats[d, i, 2:3, :] = jnp.sum(weight * prob_grad, axis=0, keepdims=True)
 
     def late_delta_step(d, i, fresh):
-        delta_step(d, i, fresh)
-        stats[d, i, 1:2, :] = jnp.ones((1, width), jnp.float32)
+        low, high = key_span(d, i)
+        prob_grad = dot_t(keys_of(d)[1][low * B : high * B, :], g_heads[i])
+        weight = probs[d, i, low * B : high * B, :].astype(jnp.float32)
+        total = jnp.sum(weight * prob_grad, axis=0, keepdims=True)
+        stats[d, i, 2:3, :] = total
+        done = jnp.logical_or(jnp.int32(d) == reach, jnp.int32(i) == nb - 1)
+        stats[d, i, 3:4, :] = jnp.where(done, jnp.float32(1.0), stats[d, i, 1:2, :])
 
     def value_step(d, i, fresh):
         low, high = key_span(d, i)
@@ -310,11 +323,7 @@
             kv_sum[d, 0, low * B : high * B, :] = term
         else:
             kv_sum[d, 0, low * B : high * B, :] += term
-        turned = dot_lt(keys, score_half)
-        if isinstance(d, int) and d == 0:
-            dq_sum[i] = turned
-        else:
-            dq_sum[i] += turned
+        dq_sum[i] += dot_lt(keys, score_half)
 
     def over_blocks(d, step):
         if d == 0:
@@ -392,141 +401,125 @@
         inverse = 1.0 / total
         for d in range(reach + 1):
             stats[d, i, 1:2, :] = parts[d] * inverse
-
-    for d in range(reach, -1, -1):
-        present(d, value_step)
-        if d > 0:
-            send_first(d, 1)
-
-    for d in range(1, reach + 1):
-
-        @pl.when(me >= reach if d == reach else me == d)
-        def _():
-            forward(d - 1, 1).wait_recv()
-            if d < reach:
-
-                @pl.when(has_next)
-                def _():
-                    forward(d, 1).start()
-
-            over_blocks(d, late_delta_step)
-
-    for i in range(nb):
-        delta[i, 0:1, :] = functools.reduce(
-            jnp.add, [stats[d, i, 1:2, :] * stats[d, i, 2:3, :] for d in range(reach + 1)]
-        )
-
-    @pl.when(me >= reach)
-    def _():
-        kv_sum[reach, 0] = jnp.zeros((rows, HEAD_WIDTH), jnp.float32)
-
-    def grads_of(i):
-        grad_step(0, i, i == nb - 1)
+            stats[d, i, 3:4, :] = parts[d] * inverse
+
+    top, second = nb - 1, nb - 2
+
+    def over_near(i, step):
+        step(0, i, i == top)
 
         def one(d, carry):
-            grad_step(d, i, i == nb - 1)
+            step(d, i, i == top)
             return carry
 
         if reach > 1:
             lax.fori_loop(1, jnp.minimum(me, reach - 1) + 1, one, 0)
 
-        @pl.when(me >= reach)
-        def _():
-            grad_step(reach, i, False)
-
+    def over_rest(d, step, count):
+        @pl.when(me >= d)
+        def _():
+            if d in (0, reach):
+                for i in range(count - 1, -1, -1):
+                    step(d, i, False)
+                return
+
+            def one(i, carry):
+                step(d, i, False)
+                return carry
+
+            lax.fori_loop(0, count, one, 0)
+
+    def finish(i):
         part = slice(i * B, (i + 1) * B)
         turned = (dq_sum[i] * scale).T.astype(jnp.bfloat16)
         for h in range(heads):
             dq_ref[part, h * HEAD_WIDTH : (h + 1) * HEAD_WIDTH] = turned[h * B : (h + 1) * B]
-        for c in range(2):
-            own = kv_sum[0, c, part, :] * scale if c == 0 else kv_sum[0, c, part, :]
-            dkv_now[part, c * HEAD_WIDTH : (c + 1) * HEAD_WIDTH] = jnp.where(
-                has_next, jnp.float32(0.0), own
-            ).astype(jnp.bfloat16)
-
-    chunks = nb
-    step_rows = rows // chunks
-
-    def term(owner, c):
-        span = pl.ds(pl.multiple_of(owner * cols, cols), cols)
-        part = slice(c * step_rows, (c + 1) * step_rows)
+
+        @pl.when(jnp.logical_not(has_next))
+        def _():
+            for c in range(2):
+                own = kv_sum[0, c, part, :] * scale if c == 0 else kv_sum[0, c, part, :]
+                dkv_now[part, c * HEAD_WIDTH : (c + 1) * HEAD_WIDTH] = own.astype(jnp.bfloat16)
+
+    half_cols = cols // 2
+
+    def term(owner, c, h, keep):
+        span = pl.ds(pl.multiple_of(owner * cols + h * half_cols, half_cols), half_cols)
+        part = slice(c * B, (c + 1) * B)
         value = dot_t(dq_ref[part, :], wq_ref[span, :])
-        value = value + dot_t(dkv_now[part, :HEAD_WIDTH], wk_ref[span, :])
-        return value + dot_t(dkv_now[part, HEAD_WIDTH:], wv_ref[span, :])
-
-    def to_pair(k, c):
+        if keep:
+            value = value + dot_t(dkv_now[part, :HEAD_WIDTH], wk_ref[span, :])
+            value = value + dot_t(dkv_now[part, HEAD_WIDTH:], wv_ref[span, :])
+        return value
+
+    def to_pair(k, c, h):
         return pltpu.make_async_remote_copy(
-            src_ref=pair_out.at[k, c],
-            dst_ref=pair_in.at[k, c],
-            send_sem=pair_send.at[k, c],
-            recv_sem=pair_recv.at[k, c],
+            src_ref=pair_out.at[k, c, h],
+            dst_ref=pair_in.at[k, c, h],
+            send_sem=pair_send.at[k, c, h],
+            recv_sem=pair_recv.at[k, c, h],
             device_id={"tp": partner},
             device_id_type=MESH_ID,
         )
 
-    def to_far(k, c):
+    def to_far(k, c, h):
         return pltpu.make_async_remote_copy(
-            src_ref=far_out.at[k - 1, c],
-            dst_ref=far_in.at[k - 1, c],
-            send_sem=far_send.at[k - 1, c],
-            recv_sem=far_recv.at[k - 1, c],
+            src_ref=far_out.at[k - 1, c, h],
+            dst_ref=far_in.at[k - 1, c, h],
+            send_sem=far_send.at[k - 1, c, h],
+            recv_sem=far_recv.at[k - 1, c, h],
             device_id={"tp": peer_of(k)},
             device_id_type=MESH_ID,
         )
 
-    def give(k, c):
-        pair_out[k, c] = term(owner_of(k, False), c).astype(jnp.bfloat16)
-        to_pair(k, c).start()
-
-    def take(k, c):
-        value = term(owner_of(k, True), c)
-        to_pair(k, c).wait_recv()
-        value = value + pair_in[k, c].astype(jnp.float32)
+    def both(step):
+        @pl.when(has_next)
+        def _():
+            step(False)
+
+        @pl.when(jnp.logical_not(has_next))
+        def _():
+            step(True)
+
+    def give(k, c, h, keep):
+        pair_out[k, c, h] = term(owner_of(k, False), c, h, keep).astype(jnp.bfloat16)
+        to_pair(k, c, h).start()
+
+    def take(k, c, h, keep):
+        value = term(owner_of(k, True), c, h, keep)
+        to_pair(k, c, h).wait_recv()
+        value = value + pair_in[k, c, h].astype(jnp.float32)
         if k == 0:
-            near_sum[c] = value
+            near_sum[c * B : (c + 1) * B, h * half_cols : (h + 1) * half_cols] = value
         else:
-            far_out[k - 1, c] = value.astype(jnp.bfloat16)
-            to_far(k, c).start()
+            far_out[k - 1, c, h] = value.astype(jnp.bfloat16)
+            to_far(k, c, h).start()
 
     def far_terms(c):
-        for k in range(1, pairs):
-            give(k, c)
-        for k in range(1, pairs):
-            take(k, c)
-
-    grads_of(nb - 1)
-    for copy in whole:
-        copy.wait()
-    far_terms(nb - 1)
-
-    if relayed:
-
-        @pl.when(has_next)
-        def _():
-            for c in (1, 0):
-                for k in range(1, pairs):
-                    fetch(k, group, c).wait_recv()
-                    relay(k, c).start()
-
-    for i in range(nb - 2, -1, -1):
-        grads_of(i)
-    for d in range(reach, 0, -1):
-        send_first(d, 0)
-    for i in range(nb - 2, -1, -1):
-        far_terms(i)
-    for d in range(reach - 1, 0, -1):
-        send_on(d, 1)
-    near = list(range(nb - 1, -1, -1))
-    give(0, near[0])
-    for n, c in enumerate(near):
-        if n + 1 < len(near):
-            give(0, near[n + 1])
-        take(0, c)
+        def step(keep):
+            for k in range(1, pairs):
+                for h in range(2):
+                    give(k, c, h, keep)
+                for h in range(2):
+                    take(k, c, h, keep)
+
+        both(step)
+
+    def near_terms():
+        def step(keep):
+            order = [(c, h) for c in range(nb - 1, -1, -1) for h in range(2)]
+            for n in range(len(order) + 2):
+                if n < len(order):
+                    give(0, *order[n], keep)
+                if n >= 2:
+                    take(0, *order[n - 2], keep)
+
+        both(step)
 
     def gather(k, m, c):
         return pltpu.make_async_remote_copy(
-            src_ref=dkv_all.at[k, 0, c] if m == 1 and k > 0 else dkv_ref.at[c],
-            dst_ref=dkv_all.at[k, m, c],
+            src_ref=dkv_all.at[c, :, slot(k, 0)] if m == 1 else dkv_all.at[c, :, slot(0, 0)],
+            dst_ref=dkv_all.at[c, :, slot(k, m)],
             send_sem=gather_send.at[k, m, c],
             recv_sem=gather_recv.at[k, m, c],
             device_id={"tp": partner if m == 1 else peer_of(k)},
@@ -537,72 +530,148 @@
         @pl.when(has_next)
         def _():
             backward(1, c).wait_recv()
-            dkv_ref[c] = (scaled(0, c) + ret_in[0, c].astype(jnp.float32)).astype(jnp.bfloat16)
+            dkv_all[c, :, 0:HEAD_WIDTH] = (scaled(0, c) + ret_in[0, c].astype(jnp.float32)).astype(jnp.bfloat16)
             for k in range(1, pairs):
                 gather(k, 0, c).start()
             gather(0, 1, c).start()
 
-    def add_terms(pairs_of):
-        for c in range(chunks):
-            part = slice(c * step_rows, (c + 1) * step_rows)
-            value = near_sum[c]
-            for grads, w in pairs_of:
-                value = value + dot_t(grads[part, :], w[...])
-            near_sum[c] = value
+    def add_terms(k, c):
+        lanes = slice(2 * k * HEAD_WIDTH, (2 * k + 2) * HEAD_WIDTH)
+        step_cols = min(256, cols)
+        for n in range(0, cols, step_cols):
+            near_sum[:, n : n + step_cols] += dot_t(dkv_all[c, :, lanes], kw_all[c, n : n + step_cols, lanes])
 
     def near_adds(c):
-        own = span_of(place)
         gather(0, 1, c).wait_recv()
-        add_terms(
-            [
-                (dkv_ref.at[c], (wk_ref, wv_ref)[c].at[own]),
-                (dkv_all.at[0, 1, c], (wk_all, wv_all)[c].at[0, 1]),
-            ]
-        )
-
-    def far_adds(c):
+        add_terms(0, c)
+
+    def far_passes(c):
         for k in range(1, pairs):
             gather(k, 0, c).wait_recv()
             gather(k, 1, c).start()
+
+    def far_adds(c):
         for k in range(1, pairs):
             gather(k, 1, c).wait_recv()
-            add_terms([(dkv_all.at[k, m, c], (wk_all, wv_all)[c].at[k, m]) for m in range(2)])
-
+            add_terms(k, c)
+
+    present(reach, value_step)
+    send_first(reach, 1)
+    over_near(top, value_step)
+
+    for d in range(1, reach + 1):
+
+        @pl.when(me >= reach if d == reach else me == d)
+        def _():
+            forward(d - 1, 1).wait_recv()
+            if d < reach:
+
+                @pl.when(has_next)
+                def _():
+                    forward(d, 1).start()
+
+            over_blocks(d, late_delta_step)
+
+    for i in range(nb):
+        delta[i, 0:1, :] = functools.reduce(
+            jnp.add, [stats[d, i, 3:4, :] * stats[d, i, 2:3, :] for d in range(reach + 1)]
+        )
+
+    over_near(top, grad_step)
+
+    @pl.when(me >= reach)
+    def _():
+        grad_step(reach, top, False)
+
+    finish(top)
+    for copy in whole:
+        copy.wait()
+    far_terms(top)
+
+    if relayed:
+
+        @pl.when(has_next)
+        def _():
+            for c in (1, 0):
+                for k in range(1, pairs):
+                    fetch(k, group, c).wait_recv()
+                    relay(k, c).start()
+
+    over_rest(reach, grad_step, top)
+    send_first(reach, 0)
+    if reach > 1:
+        over_rest(reach - 1, value_step, top)
+        send_first(reach - 1, 1)
+
+    def rest_value(d, i, fresh):
+        if isinstance(d, int):
+            value_step(d, i, fresh)
+        else:
+
+            @pl.when(d < reach - 1)
+            def _():
+                value_step(d, i, fresh)
+
+    over_near(second, rest_value)
+    over_near(second, grad_step)
+    finish(second)
+    far_terms(second)
+    if reach > 2:
+        send_on(reach - 1, 1)
+    for d in range(reach - 2, 0, -1):
+        over_rest(d, value_step, second)
+        send_first(d, 1)
+    for d in range(reach - 1, 0, -1):
+        over_rest(d, grad_step, second)
+        send_first(d, 0)
+    over_rest(0, value_step, second)
+    over_rest(0, grad_step, second)
+    for i in range(second - 1, -1, -1):
+        finish(i)
+        far_terms(i)
+    for d in range(reach - 2, 1, -1):
+        send_on(d, 1)
+    for d in range(reach - 1, 1, -1):
+        send_on(d, 0)
+    near_terms()
+    if reach > 1:
+        send_on(1, 1)
+        send_on(1, 0)
     settle(1)
 
     @pl.when(has_next)
     def _():
         for c in range(2):
+            own_weights(c).wait()
             fetch(0, 1, c).wait_recv()
         near_adds(1)
 
-    for d in range(reach - 1, 0, -1):
-        send_on(d, 0)
+    settle(0)
 
     @pl.when(has_next)
     def _():
         for k in range(1, pairs):
             for c in range(2):
                 if relayed:
-                    relay_in(k, c).wait_recv()
+                    relay(k, c, True).wait_recv()
                 else:
                     for m in range(2):
                         fetch(k, m, c).wait_recv()
+        far_passes(1)
+        near_adds(0)
         far_adds(1)
-
-    settle(0)
-
-    @pl.when(has_next)
-    def _():
-        near_adds(0)
+        far_passes(0)
         far_adds(0)
 
+    near = list(range(nb - 1, -1, -1))
     for c in near:
-        value = near_sum[c]
-        for k in range(1, pairs):
-            to_far(k, c).wait_recv()
-            value = value + far_in[k - 1, c].astype(jnp.float32)
-        out_ref[c * step_rows : (c + 1) * step_rows, :] = value.astype(jnp.bfloat16)
+        for h in range(2):
+            part = (slice(c * B, (c + 1) * B), slice(h * half_cols, (h + 1) * half_cols))
+            value = near_sum[part]
+            for k in range(1, pairs):
+                to_far(k, c, h).wait_recv()
+                value = value + far_in[k - 1, c, h].astype(jnp.float32)
+            out_ref[part] = value.astype(jnp.bfloat16)
 
     @pl.when(has_next)
     def _():
@@ -617,10 +686,11 @@
                     relay(k, c).wait_send()
 
     for c in near:
-        for k in range(pairs):
-            to_pair(k, c).wait_send()
-            if k > 0:
-                to_far(k, c).wait_send()
+        for h in range(2):
+            for k in range(pairs):
+                to_pair(k, c, h).wait_send()
+                if k > 0:
+                    to_far(k, c, h).wait_send()
 
     for d in range(reach):
 
@@ -664,19 +734,17 @@
         ((rows, HEAD_WIDTH), half),
         ((rows, q_width), half),
         ((rows, q_width), half),
-        ((2, rows, HEAD_WIDTH), half),
         ((rows, 2 * HEAD_WIDTH), half),
-        ((pairs, 2, 2, rows, HEAD_WIDTH), half),
-        ((pairs, 2, cols, HEAD_WIDTH), half),
-        ((pairs, 2, cols, HEAD_WIDTH), half),
+        ((2, rows, 2 * pairs * HEAD_WIDTH), half),
+        ((2, cols, 2 * pairs * HEAD_WIDTH), half),
         (w_query.shape, half),
         (key_weight.shape, half),
         (value_weight.shape, half),
-        ((nb, rows // nb, cols), full),
-        ((pairs, nb, rows // nb, cols), half),
-        ((pairs, nb, rows // nb, cols), half),
-        ((pairs - 1, nb, rows // nb, cols), half),
-        ((pairs - 1, nb, rows // nb, cols), half),
+        ((rows, cols), full),
+        ((pairs, nb, 2, rows // nb, cols // 2), half),
+        ((pairs, nb, 2, rows // nb, cols // 2), half),
+        ((pairs - 1, nb, 2, rows // nb, cols // 2), half),
+        ((pairs - 1, nb, 2, rows // nb, cols // 2), half),
     ]
     later = [
         ((reach, 2, rows, HEAD_WIDTH), half),
@@ -695,16 +763,17 @@
     return pl.pallas_call(
         functools.partial(attention_kernel, shards, reach, places, groups),
         out_shape=jax.ShapeDtypeStruct((rows, cols), half),
-        in_specs=[hbm] * 4 + [pl.BlockSpec(memory_space=pltpu.SMEM)] + [hbm] * 3,
+        in_specs=[hbm] * 8,
         out_specs=vmem,
-        scratch_shapes=[pltpu.VMEM(*item) for item in buffers]
+        scratch_shapes=[pltpu.SMEM(doc_blocks.shape, doc_blocks.dtype)]
+        + [pltpu.VMEM(*item) for item in buffers]
         + [
-            dma((4,)),
+            dma((5,)),
             dma((3,)),
-            dma((pairs, nb)),
-            dma((pairs, nb)),
-            dma((pairs - 1, nb)),
-            dma((pairs - 1, nb)),
+            dma((pairs, nb, 2)),
+            dma((pairs, nb, 2)),
+            dma((pairs - 1, nb, 2)),
+            dma((pairs - 1, nb, 2)),
             dma((pairs, 2, 2)),
             dma((pairs, 2, 2)),
             dma((pairs, 2)),
@@ -728,7 +797,7 @@
         pltpu.with_memory_space_constraint(key_head_rows, pltpu.HBM),
         pltpu.with_memory_space_constraint(value_head_rows, pltpu.HBM),
         pltpu.with_memory_space_constraint(output_gradient, pltpu.HBM),
-        doc_blocks,
+        pltpu.with_memory_space_constraint(doc_blocks, pltpu.HBM),
         pltpu.with_memory_space_constraint(w_query, pltpu.HBM),
         pltpu.with_memory_space_constraint(key_weight, pltpu.HBM),
         pltpu.with_memory_space_constraint(value_weight, pltpu.HBM),

time: 63.2 us -> 56.7 us (0.90)
  the two profiles are of different devices: /device:TPU:1 before, /device:TPU:9 now
where the time goes in v2:
time: 56.7 us; the launch traced here: 56.6 us
  Pallas kernels  55.6 us (98%)
  local copies, waits for them, and re-layouts  0.97 us (2%)
    pallas_call x1, Pallas kernels, body(): pl.pallas_call(functools.partial(attention_kernel, shards, reach, places,...  55.6 us

profile of v2, /device:TPU:9, one launch (start us, length us, event | category | flops | bytes accessed | tf_op | source)
XLA Modules:
  0.0 56.6 jit_solution(9442277736464424393)
XLA Ops:
  0.0 55.6 %attention.1 = bf16[512,1024]{1,0:T(8,128)(2,1)S(1)} custom-call(bf16[512,512]{1,0:T(8,128)(2,1)} %q_hbm.1, bf16[512,128]{1,0:T(8,128)(2,1)} %k_hbm.1, bf16[512,128]{1,0:T(8,128)(2,1)} %v_hbm.1, bf16[512,512]{1,0:T(8,128)(2,1)} %g_hbm.1, s32[4,8]{1,0:T(4,128)} %docs_hbm.1, bf16[4096,512]{1,0:T(8,128)(2,1)} %wq_hbm.1, bf16[4096,128]{1,0:T(8,128)(2,1)} %wk_hbm.1, ...), custom_call_target="tpu_custom_call" | custom-call | tf_op jit(solution)/shard_map/attention/pallas_call | solution.py:763
  55.6 1.0 %copy.10 = bf16[512,1024]{1,0:T(8,128)(2,1)} copy(bf16[512,1024]{1,0:T(8,128)(2,1)S(1)} %attention.1) | data formatting | bytes 2097152

commit v3 on v2

--- a/solution.py
+++ b/solution.py
@@ -56,12 +56,16 @@
     wk_ref,
     wv_ref,
     near_sum,
+    near_out,
+    near_in,
     pair_out,
     pair_in,
     far_out,
     far_in,
     load_sem,
     weight_sem,
+    near_send,
+    near_recv,
     pair_send,
     pair_recv,
     far_send,
@@ -204,7 +208,11 @@
     @pl.when(has_next)
     def _():
         forward(0, 0).start()
-        forward(0, 1).start()
+
+        @pl.when(me != 1)
+        def _():
+            forward(0, 1).start()
+
         for item in fetches:
             fetch(*item).start()
         for c in range(2):
@@ -292,14 +300,13 @@
         weight = probs[d, i, low * B : high * B, :].astype(jnp.float32)
         stats[d, i, 2:3, :] = jnp.sum(weight * prob_grad, axis=0, keepdims=True)
 
-    def late_delta_step(d, i, fresh):
-        low, high = key_span(d, i)
-        prob_grad = dot_t(keys_of(d)[1][low * B : high * B, :], g_heads[i])
-        weight = probs[d, i, low * B : high * B, :].astype(jnp.float32)
-        total = jnp.sum(weight * prob_grad, axis=0, keepdims=True)
-        stats[d, i, 2:3, :] = total
-        done = jnp.logical_or(jnp.int32(d) == reach, jnp.int32(i) == nb - 1)
-        stats[d, i, 3:4, :] = jnp.where(done, jnp.float32(1.0), stats[d, i, 1:2, :])
+    def scaled_delta_step(whole_from):
+        def step(d, i, fresh):
+            delta_step(d, i, fresh)
+            done = jnp.logical_or(jnp.int32(d) >= whole_from, jnp.int32(i) == nb - 1)
+            stats[d, i, 3:4, :] = jnp.where(done, jnp.float32(1.0), stats[d, i, 1:2, :])
+
+        return step
 
     def value_step(d, i, fresh):
         low, high = key_span(d, i)
@@ -347,17 +354,29 @@
         def _():
             over_blocks(d, step)
 
-    def arrive(d, c):
-        @pl.when(me >= d)
+    def arrive(d, c, checked=True):
+        there = me >= d if checked else True
+
+        @pl.when(there)
         def _():
             forward(d - 1, c).wait_recv()
 
         if d < reach:
 
-            @pl.when((me >= d) & has_next)
+            @pl.when(there & has_next)
             def _():
                 forward(d, c).start()
 
+        if d == 1 and c == 0:
+
+            @pl.when((me == 1) & has_next)
+            def _():
+                forward(0, 1).start()
+
+    def take_values(d, step):
+        arrive(d, 1, False)
+        over_blocks(d, step)
+
     def scaled(d, c):
         return kv_sum[d, c] * scale if c == 0 else kv_sum[d, c]
 
@@ -369,8 +388,8 @@
             ret_out[d - 1, c] = scaled(d, c).astype(jnp.bfloat16)
             backward(d, c).start()
 
-    def send_on(d, c):
-        @pl.when((me >= d) & has_next)
+    def send_on(d, c, extra=None):
+        @pl.when((me >= d if extra is None else extra) & has_next)
         def _():
             backward(d + 1, c).wait_recv()
             ret_out[d - 1, c] = (scaled(d, c) + ret_in[d, c].astype(jnp.float32)).astype(jnp.bfloat16)
@@ -383,15 +402,9 @@
         present(d, score_step)
         if d < reach:
 
-            @pl.when(me > d)
+            @pl.when(me > d + 1)
             def _():
-                forward(d - 1, 1).wait_recv()
-
-                @pl.when(has_next)
-                def _():
-                    forward(d, 1).start()
-
-                over_blocks(d, delta_step)
+                take_values(d, delta_step)
 
     for i in range(nb):
         tops = [stats[d, i, 0:1, :] for d in range(reach + 1)]
@@ -415,19 +428,31 @@
         if reach > 1:
             lax.fori_loop(1, jnp.minimum(me, reach - 1) + 1, one, 0)
 
+    def rest_value(d, i, fresh):
+        if isinstance(d, int):
+            value_step(d, i, fresh)
+        else:
+
+            @pl.when(d < reach - 1)
+            def _():
+                value_step(d, i, fresh)
+
+    def rest_blocks(d, step, count):
+        if d in (0, reach):
+            for i in range(count - 1, -1, -1):
+                step(d, i, False)
+            return
+
+        def one(i, carry):
+            step(d, i, False)
+            return carry
+
+        lax.fori_loop(0, count, one, 0)
+
     def over_rest(d, step, count):
         @pl.when(me >= d)
         def _():
-            if d in (0, reach):
-                for i in range(count - 1, -1, -1):
-                    step(d, i, False)
-                return
-
-            def one(i, carry):
-                step(d, i, False)
-                return carry
-
-            lax.fori_loop(0, count, one, 0)
+            rest_blocks(d, step, count)
 
     def finish(i):
         part = slice(i * B, (i + 1) * B)
@@ -442,10 +467,11 @@
                 dkv_now[part, c * HEAD_WIDTH : (c + 1) * HEAD_WIDTH] = own.astype(jnp.bfloat16)
 
     half_cols = cols // 2
-
-    def term(owner, c, h, keep):
-        span = pl.ds(pl.multiple_of(owner * cols + h * half_cols, half_cols), half_cols)
-        part = slice(c * B, (c + 1) * B)
+    piece = math.gcd(cols, 256)
+    hold = me + 2 == shards
+
+    def term(owner, part, first, count, keep):
+        span = pl.ds(pl.multiple_of(owner * cols + first, count), count)
         value = dot_t(dq_ref[part, :], wq_ref[span, :])
         if keep:
             value = value + dot_t(dkv_now[part, :HEAD_WIDTH], wk_ref[span, :])
@@ -454,10 +480,10 @@
 
     def to_pair(k, c, h):
         return pltpu.make_async_remote_copy(
-            src_ref=pair_out.at[k, c, h],
-            dst_ref=pair_in.at[k, c, h],
-            send_sem=pair_send.at[k, c, h],
-            recv_sem=pair_recv.at[k, c, h],
+            src_ref=pair_out.at[k - 1, c, h],
+            dst_ref=pair_in.at[k - 1, c, h],
+            send_sem=pair_send.at[k - 1, c, h],
+            recv_sem=pair_recv.at[k - 1, c, h],
             device_id={"tp": partner},
             device_id_type=MESH_ID,
         )
@@ -472,6 +498,16 @@
             device_id_type=MESH_ID,
         )
 
+    def to_near(n):
+        return pltpu.make_async_remote_copy(
+            src_ref=near_out.at[n],
+            dst_ref=near_in.at[n],
+            send_sem=near_send.at[n],
+            recv_sem=near_recv.at[n],
+            device_id={"tp": partner},
+            device_id_type=MESH_ID,
+        )
+
     def both(step):
         @pl.when(has_next)
         def _():
@@ -481,38 +517,45 @@
         def _():
             step(True)
 
-    def give(k, c, h, keep):
-        pair_out[k, c, h] = term(owner_of(k, False), c, h, keep).astype(jnp.bfloat16)
-        to_pair(k, c, h).start()
-
-    def take(k, c, h, keep):
-        value = term(owner_of(k, True), c, h, keep)
-        to_pair(k, c, h).wait_recv()
-        value = value + pair_in[k, c, h].astype(jnp.float32)
-        if k == 0:
-            near_sum[c * B : (c + 1) * B, h * half_cols : (h + 1) * half_cols] = value
-        else:
-            far_out[k - 1, c, h] = value.astype(jnp.bfloat16)
-            to_far(k, c, h).start()
-
-    def far_terms(c):
+    def far_terms(low, count):
+        part = slice(low * B, (low + count) * B)
+
         def step(keep):
             for k in range(1, pairs):
                 for h in range(2):
-                    give(k, c, h, keep)
+                    value = term(owner_of(k, False), part, h * half_cols, half_cols, keep).astype(jnp.bfloat16)
+                    for n in range(count - 1, -1, -1):
+                        pair_out[k - 1, low + n, h] = value[n * B : (n + 1) * B]
+                        to_pair(k, low + n, h).start()
                 for h in range(2):
-                    take(k, c, h, keep)
+                    value = term(owner_of(k, True), part, h * half_cols, half_cols, keep)
+                    for n in range(count - 1, -1, -1):
+                        c = low + n
+                        to_pair(k, c, h).wait_recv()
+                        total = value[n * B : (n + 1) * B] + pair_in[k - 1, c, h].astype(jnp.float32)
+                        far_out[k - 1, c, h] = total.astype(jnp.bfloat16)
+                        if keep or (c, h) != (0, 1):
+                            to_far(k, c, h).start()
+                        else:
+
+                            @pl.when(jnp.logical_not(hold))
+                            def _():
+                                to_far(k, c, h).start()
 
         both(step)
 
     def near_terms():
         def step(keep):
-            order = [(c, h) for c in range(nb - 1, -1, -1) for h in range(2)]
-            for n in range(len(order) + 2):
-                if n < len(order):
-                    give(0, *order[n], keep)
+            part = slice(0, rows)
+            count = cols // piece
+            for n in range(count + 2):
+                if n < count:
+                    near_out[n] = term(partner, part, n * piece, piece, keep).astype(jnp.bfloat16)
+                    to_near(n).start()
                 if n >= 2:
-                    take(0, *order[n - 2], keep)
+                    value = term(place, part, (n - 2) * piece, piece, keep)
+                    to_near(n - 2).wait_recv()
+                    near_sum[:, (n - 2) * piece : (n - 1) * piece] = value + near_in[n - 2].astype(jnp.float32)
 
         both(step)
 
@@ -559,24 +602,26 @@
     send_first(reach, 1)
     over_near(top, value_step)
 
+    for d in range(1, reach):
+
+        @pl.when(me == d + 1)
+        def _():
+            take_values(d, scaled_delta_step(reach))
+
+    late_step = scaled_delta_step(reach)
     for d in range(1, reach + 1):
 
         @pl.when(me >= reach if d == reach else me == d)
         def _():
-            forward(d - 1, 1).wait_recv()
-            if d < reach:
-
-                @pl.when(has_next)
-                def _():
-                    forward(d, 1).start()
-
-            over_blocks(d, late_delta_step)
-
-    for i in range(nb):
+            arrive(d, 1, False)
+            late_step(d, top, False)
+
+    def sum_delta(i):
         delta[i, 0:1, :] = functools.reduce(
             jnp.add, [stats[d, i, 3:4, :] * stats[d, i, 2:3, :] for d in range(reach + 1)]
         )
 
+    sum_delta(top)
     over_near(top, grad_step)
 
     @pl.when(me >= reach)
@@ -586,7 +631,7 @@
     finish(top)
     for copy in whole:
         copy.wait()
-    far_terms(top)
+    far_terms(top, 1)
 
     if relayed:
 
@@ -597,47 +642,45 @@
                     fetch(k, group, c).wait_recv()
                     relay(k, c).start()
 
+    for d in range(1, reach + 1):
+
+        @pl.when(me >= reach if d == reach else me == d)
+        def _():
+            rest_blocks(d, late_step, top)
+
+    for i in range(top):
+        sum_delta(i)
     over_rest(reach, grad_step, top)
     send_first(reach, 0)
     if reach > 1:
         over_rest(reach - 1, value_step, top)
         send_first(reach - 1, 1)
-
-    def rest_value(d, i, fresh):
-        if isinstance(d, int):
-            value_step(d, i, fresh)
-        else:
-
-            @pl.when(d < reach - 1)
-            def _():
-                value_step(d, i, fresh)
-
     over_near(second, rest_value)
     over_near(second, grad_step)
     finish(second)
-    far_terms(second)
-    if reach > 2:
-        send_on(reach - 1, 1)
+    far_terms(second, 1)
     for d in range(reach - 2, 0, -1):
         over_rest(d, value_step, second)
         send_first(d, 1)
+    over_rest(0, value_step, second)
+    for d in range(reach - 1, 1, -1):
+        send_on(d, 1)
     for d in range(reach - 1, 0, -1):
         over_rest(d, grad_step, second)
         send_first(d, 0)
-    over_rest(0, value_step, second)
     over_rest(0, grad_step, second)
-    for i in range(second - 1, -1, -1):
+    for i in range(second):
         finish(i)
-        far_terms(i)
-    for d in range(reach - 2, 1, -1):
-        send_on(d, 1)
+    far_terms(0, second)
     for d in range(reach - 1, 1, -1):
         send_on(d, 0)
     near_terms()
     if reach > 1:
         send_on(1, 1)
-        send_on(1, 0)
+        send_on(1, 0, me == 1)
     settle(1)
+    if reach > 1:
+        send_on(1, 0, me >= 2)
 
     @pl.when(has_next)
     def _():
@@ -650,6 +693,11 @@
 
     @pl.when(has_next)
     def _():
+        @pl.when(hold)
+        def _():
+            for k in range(1, pairs):
+                to_far(k, 0, 1).start()
+
         for k in range(1, pairs):
             for c in range(2):
                 if relayed:
@@ -687,10 +735,11 @@
 
     for c in near:
         for h in range(2):
-            for k in range(pairs):
+            for k in range(1, pairs):
                 to_pair(k, c, h).wait_send()
-                if k > 0:
-                    to_far(k, c, h).wait_send()
+                to_far(k, c, h).wait_send()
+    for n in range(cols // piece):
+        to_near(n).wait_send()
 
     for d in range(reach):
 
@@ -741,8 +790,10 @@
         (key_weight.shape, half),
         (value_weight.shape, half),
         ((rows, cols), full),
-        ((pairs, nb, 2, rows // nb, cols // 2), half),
-        ((pairs, nb, 2, rows // nb, cols // 2), half),
+        ((cols // math.gcd(cols, 256), rows, math.gcd(cols, 256)), half),
+        ((cols // math.gcd(cols, 256), rows, math.gcd(cols, 256)), half),
+        ((pairs - 1, nb, 2, rows // nb, cols // 2), half),
+        ((pairs - 1, nb, 2, rows // nb, cols // 2), half),
         ((pairs - 1, nb, 2, rows // nb, cols // 2), half),
         ((pairs - 1, nb, 2, rows // nb, cols // 2), half),
     ]
@@ -770,8 +821,10 @@
         + [
             dma((5,)),
             dma((3,)),
-            dma((pairs, nb, 2)),
-            dma((pairs, nb, 2)),
+            dma((cols // math.gcd(cols, 256),)),
+            dma((cols // math.gcd(cols, 256),)),
+            dma((pairs - 1, nb, 2)),
+            dma((pairs - 1, nb, 2)),
             dma((pairs - 1, nb, 2)),
             dma((pairs - 1, nb, 2)),
             dma((pairs, 2, 2)),

time: 56.7 us -> 54.1 us (0.954)
  Pallas kernels: 55.6 us -> 53 us
    pallas_call x1, Pallas kernels: 55.6 us -> 53 us  [body(): pl.pallas_call(functools.partial(attention_kernel, shards, reach, places,...]
where the time goes in v3:
time: 54.1 us; the launch traced here: 54 us
  Pallas kernels  53 us (98%)
  local copies, waits for them, and re-layouts  0.97 us (2%)
    pallas_call x1, Pallas kernels, body(): pl.pallas_call(functools.partial(attention_kernel, shards, reach, places,...  53 us

profile of v3, /device:TPU:9, one launch (start us, length us, event | category | flops | bytes accessed | tf_op | source)
XLA Modules:
  0.0 54.0 jit_solution(7914777153020196161)
XLA Ops:
  0.0 53.0 %attention.1 = bf16[512,1024]{1,0:T(8,128)(2,1)S(1)} custom-call(bf16[512,512]{1,0:T(8,128)(2,1)} %q_hbm.1, bf16[512,128]{1,0:T(8,128)(2,1)} %k_hbm.1, bf16[512,128]{1,0:T(8,128)(2,1)} %v_hbm.1, bf16[512,512]{1,0:T(8,128)(2,1)} %g_hbm.1, s32[4,8]{1,0:T(4,128)} %docs_hbm.1, bf16[4096,512]{1,0:T(8,128)(2,1)} %wq_hbm.1, bf16[4096,128]{1,0:T(8,128)(2,1)} %wk_hbm.1, ...), custom_call_target="tpu_custom_call" | custom-call | tf_op jit(solution)/shard_map/attention/pallas_call | solution.py:814
  53.0 1.0 %copy.10 = bf16[512,1024]{1,0:T(8,128)(2,1)} copy(bf16[512,1024]{1,0:T(8,128)(2,1)S(1)} %attention.1) | data formatting | bytes 2097152

commit v4 on v3

--- a/solution.py
+++ b/solution.py
@@ -49,7 +49,7 @@
     v_ref,
     g_ref,
     dq_ref,
-    dkv_now,
+    turned_ref,
     dkv_all,
     kw_all,
     wq_ref,
@@ -88,6 +88,8 @@
     ret_in,
     send_sem,
     recv_sem,
+    last_send,
+    last_recv,
     ret_send,
     ret_recv,
 ):
@@ -95,6 +97,7 @@
     rows = k_ref.shape[0]
     nb = rows // B
     heads = q_ref.shape[1] // HEAD_WIDTH
+    lead = q_ref.shape[1]
     listed_count = docs_ref.shape[1]
     me = lax.axis_index("seq")
     scale = HEAD_WIDTH ** -0.5
@@ -121,7 +124,12 @@
         pltpu.make_async_copy(src, dst, load_sem.at[n])
         for n, (src, dst) in enumerate(((k_hbm, k_ref), (q_hbm, q_ref), (v_hbm, v_ref), (g_hbm, g_ref), (docs_hbm, docs_ref)))
     ]
-    for copy in loads:
+    whole = [
+        pltpu.make_async_copy(wq_hbm, wq_ref, weight_sem.at[0]),
+        pltpu.make_async_copy(wk_hbm, wk_ref, weight_sem.at[1]),
+        pltpu.make_async_copy(wv_hbm, wv_ref, weight_sem.at[2]),
+    ]
+    for copy in loads + whole:
         copy.start()
 
     barrier = pltpu.get_barrier_semaphore()
@@ -149,6 +157,17 @@
             dst_ref=kv_win.at[d, c],
             send_sem=send_sem.at[d, c],
             recv_sem=recv_sem.at[d, c],
+            device_id={"seq": jnp.minimum(me + 1, shards - 1)},
+            device_id_type=MESH_ID,
+        )
+
+    def last_hop(n):
+        span = pl.ds(rows - B, B) if n == 0 else pl.ds(0, rows - B)
+        return pltpu.make_async_remote_copy(
+            src_ref=(v_hbm if reach == 1 else kv_win.at[reach - 2, 1]).at[span],
+            dst_ref=kv_win.at[reach - 1, 1, span],
+            send_sem=last_send.at[n],
+            recv_sem=last_recv.at[n],
             device_id={"seq": jnp.minimum(me + 1, shards - 1)},
             device_id_type=MESH_ID,
         )
@@ -218,14 +237,6 @@
         for c in range(2):
             own_weights(c).start()
 
-    whole = [
-        pltpu.make_async_copy(wq_hbm, wq_ref, weight_sem.at[0]),
-        pltpu.make_async_copy(wk_hbm, wk_ref, weight_sem.at[1]),
-        pltpu.make_async_copy(wv_hbm, wv_ref, weight_sem.at[2]),
-    ]
-    for copy in whole:
-        copy.start()
-
     width = heads * B
     for d in range(1, reach + 1):
         for i in range(nb):
@@ -359,19 +370,20 @@
 
         @pl.when(there)
         def _():
-            forward(d - 1, c).wait_recv()
+            if (d, c) == (reach, 1):
+                last_hop(0).wait_recv()
+            else:
+                forward(d - 1, c).wait_recv()
 
         if d < reach:
 
             @pl.when(there & has_next)
             def _():
-                forward(d, c).start()
-
-        if d == 1 and c == 0:
-
-            @pl.when((me == 1) & has_next)
-            def _():
-                forward(0, 1).start()
+                if (d, c) == (reach - 1, 1):
+                    last_hop(0).start()
+                    last_hop(1).start()
+                else:
+                    forward(d, c).start()
 
     def take_values(d, step):
         arrive(d, 1, False)
@@ -380,8 +392,8 @@
     def scaled(d, c):
         return kv_sum[d, c] * scale if c == 0 else kv_sum[d, c]
 
-    def send_first(d, c):
-        first = me >= d if d == reach else (me >= d) & jnp.logical_not(has_next)
+    def send_first(d, c, extra=True):
+        first = me >= d if d == reach else (me >= d) & jnp.logical_not(has_next) & extra
 
         @pl.when(first)
         def _():
@@ -397,9 +409,36 @@
 
     present(0, score_step)
     present(0, delta_step)
+    for copy in whole:
+        copy.wait()
+    for k in range(1, pairs):
+        for m in range(2):
+            span = span_of(owner_of(k, m == 0))
+            turned_ref[k - 1, m, :lead, :] = wq_ref[span, :].T
+
+    @pl.when(jnp.logical_not(has_next))
+    def _():
+        for k in range(1, pairs):
+            for m in range(2):
+                span = span_of(owner_of(k, m == 0))
+                turned_ref[k - 1, m, lead : lead + HEAD_WIDTH, :] = wk_ref[span, :].T
+                turned_ref[k - 1, m, lead + HEAD_WIDTH :, :] = wv_ref[span, :].T
+
     for d in range(1, reach + 1):
         arrive(d, 0)
+        if d == 1:
+
+            @pl.when((me == 1) & (parity == 0) & has_next)
+            def _():
+                forward(0, 1).start()
+
         present(d, score_step)
+        if d == 1:
+
+            @pl.when((me == 1) & (parity == 1) & has_next)
+            def _():
+                forward(0, 1).start()
+
         if d < reach:
 
             @pl.when(me > d + 1)
@@ -428,15 +467,6 @@
         if reach > 1:
             lax.fori_loop(1, jnp.minimum(me, reach - 1) + 1, one, 0)
 
-    def rest_value(d, i, fresh):
-        if isinstance(d, int):
-            value_step(d, i, fresh)
-        else:
-
-            @pl.when(d < reach - 1)
-            def _():
-                value_step(d, i, fresh)
-
     def rest_blocks(d, step, count):
         if d in (0, reach):
             for i in range(count - 1, -1, -1):
@@ -464,19 +494,23 @@
         def _():
             for c in range(2):
                 own = kv_sum[0, c, part, :] * scale if c == 0 else kv_sum[0, c, part, :]
-                dkv_now[part, c * HEAD_WIDTH : (c + 1) * HEAD_WIDTH] = own.astype(jnp.bfloat16)
+                dq_ref[part, lead + c * HEAD_WIDTH : lead + (c + 1) * HEAD_WIDTH] = own.astype(jnp.bfloat16)
 
     half_cols = cols // 2
-    piece = math.gcd(cols, 256)
+    piece = math.gcd(cols, 512)
     hold = me + 2 == shards
 
     def term(owner, part, first, count, keep):
         span = pl.ds(pl.multiple_of(owner * cols + first, count), count)
-        value = dot_t(dq_ref[part, :], wq_ref[span, :])
+        value = dot_t(dq_ref[part, :lead], wq_ref[span, :])
         if keep:
-            value = value + dot_t(dkv_now[part, :HEAD_WIDTH], wk_ref[span, :])
-            value = value + dot_t(dkv_now[part, HEAD_WIDTH:], wv_ref[span, :])
+            value = value + dot_t(dq_ref[part, lead : lead + HEAD_WIDTH], wk_ref[span, :])
+            value = value + dot_t(dq_ref[part, lead + HEAD_WIDTH :], wv_ref[span, :])
         return value
+
+    def far_term(k, m, part, keep):
+        depth = lead + 2 * HEAD_WIDTH if keep else lead
+        return dot_n(dq_ref[part, :depth], turned_ref[k - 1, m, :depth, :])
 
     def to_pair(k, c, h):
         return pltpu.make_async_remote_copy(
@@ -517,22 +551,31 @@
         def _():
             step(True)
 
-    def far_terms(low, count):
+    def far_give(low, count):
         part = slice(low * B, (low + count) * B)
 
         def step(keep):
             for k in range(1, pairs):
-                for h in range(2):
-                    value = term(owner_of(k, False), part, h * half_cols, half_cols, keep).astype(jnp.bfloat16)
-                    for n in range(count - 1, -1, -1):
-                        pair_out[k - 1, low + n, h] = value[n * B : (n + 1) * B]
+                value = far_term(k, 1, part, keep).astype(jnp.bfloat16)
+                for n in range(count - 1, -1, -1):
+                    for h in range(2):
+                        pair_out[k - 1, low + n, h] = value[n * B : (n + 1) * B, h * half_cols : (h + 1) * half_cols]
                         to_pair(k, low + n, h).start()
-                for h in range(2):
-                    value = term(owner_of(k, True), part, h * half_cols, half_cols, keep)
-                    for n in range(count - 1, -1, -1):
+
+        both(step)
+
+    def far_take(low, count, which):
+        part = slice(low * B, (low + count) * B)
+
+        def step(keep):
+            for k in range(1, pairs):
+                value = far_term(k, 0, part, keep)
+                for n in range(count - 1, -1, -1):
+                    for h in range(2):
                         c = low + n
                         to_pair(k, c, h).wait_recv()
-                        total = value[n * B : (n + 1) * B] + pair_in[k - 1, c, h].astype(jnp.float32)
+                        total = value[n * B : (n + 1) * B, h * half_cols : (h + 1) * half_cols]
+                        total = total + pair_in[k - 1, c, h].astype(jnp.float32)
                         far_out[k - 1, c, h] = total.astype(jnp.bfloat16)
                         if keep or (c, h) != (0, 1):
                             to_far(k, c, h).start()
@@ -542,20 +585,24 @@
                             def _():
                                 to_far(k, c, h).start()
 
+        @pl.when(parity == which)
+        def _():
+            both(step)
+
+    def near_give():
+        def step(keep):
+            for n in range(cols // piece):
+                near_out[n] = term(partner, slice(0, rows), n * piece, piece, keep).astype(jnp.bfloat16)
+                to_near(n).start()
+
         both(step)
 
-    def near_terms():
+    def near_take():
         def step(keep):
-            part = slice(0, rows)
-            count = cols // piece
-            for n in range(count + 2):
-                if n < count:
-                    near_out[n] = term(partner, part, n * piece, piece, keep).astype(jnp.bfloat16)
-                    to_near(n).start()
-                if n >= 2:
-                    value = term(place, part, (n - 2) * piece, piece, keep)
-                    to_near(n - 2).wait_recv()
-                    near_sum[:, (n - 2) * piece : (n - 1) * piece] = value + near_in[n - 2].astype(jnp.float32)
+            for n in range(cols // piece):
+                value = term(place, slice(0, rows), n * piece, piece, keep)
+                to_near(n).wait_recv()
+                near_sum[:, n * piece : (n + 1) * piece] = value + near_in[n].astype(jnp.float32)
 
         both(step)
 
@@ -569,8 +616,8 @@
             device_id_type=MESH_ID,
         )
 
-    def settle(c):
-        @pl.when(has_next)
+    def settle(c, extra=True):
+        @pl.when(has_next & extra)
         def _():
             backward(1, c).wait_recv()
             dkv_all[c, :, 0:HEAD_WIDTH] = (scaled(0, c) + ret_in[0, c].astype(jnp.float32)).astype(jnp.bfloat16)
@@ -602,19 +649,33 @@
     send_first(reach, 1)
     over_near(top, value_step)
 
-    for d in range(1, reach):
-
-        @pl.when(me == d + 1)
-        def _():
-            take_values(d, scaled_delta_step(reach))
-
-    late_step = scaled_delta_step(reach)
-    for d in range(1, reach + 1):
-
-        @pl.when(me >= reach if d == reach else me == d)
-        def _():
-            arrive(d, 1, False)
-            late_step(d, top, False)
+
+    for d in range(reach - 1, 0, -1):
+
+        @pl.when(me >= reach)
+        def _():
+            rest_blocks(d, value_step, top)
+
+        send_first(d, 1)
+
+    def late_deltas(step):
+        for d in range(1, reach):
+
+            @pl.when(me == d + 1)
+            def _():
+                step(d, scaled_delta_step(reach - 1 if d == reach - 1 else reach))
+
+        for d in range(1, reach + 1):
+
+            @pl.when(me >= reach if d == reach else me == d)
+            def _():
+                step(d, scaled_delta_step(reach))
+
+    def late_top(d, step):
+        arrive(d, 1, False)
+        step(d, top, False)
+
+    late_deltas(late_top)
 
     def sum_delta(i):
         delta[i, 0:1, :] = functools.reduce(
@@ -629,9 +690,8 @@
         grad_step(reach, top, False)
 
     finish(top)
-    for copy in whole:
-        copy.wait()
-    far_terms(top, 1)
+    far_give(top, 1)
+    far_take(top, 1, 0)
 
     if relayed:
 
@@ -642,45 +702,64 @@
                     fetch(k, group, c).wait_recv()
                     relay(k, c).start()
 
-    for d in range(1, reach + 1):
-
-        @pl.when(me >= reach if d == reach else me == d)
-        def _():
-            rest_blocks(d, late_step, top)
-
+    def late_rest(d, step):
+        if d == reach:
+
+            @pl.when(me >= reach)
+            def _():
+                last_hop(1).wait_recv()
+
+        rest_blocks(d, step, top)
+
+    def second_value(d, i, fresh):
+        if isinstance(d, int):
+            value_step(d, i, fresh)
+        else:
+
+            @pl.when(me < reach)
+            def _():
+                value_step(d, i, fresh)
+
+    late_deltas(late_rest)
     for i in range(top):
         sum_delta(i)
     over_rest(reach, grad_step, top)
     send_first(reach, 0)
-    if reach > 1:
-        over_rest(reach - 1, value_step, top)
-        send_first(reach - 1, 1)
-    over_near(second, rest_value)
+    far_take(top, 1, 1)
+    over_near(second, second_value)
     over_near(second, grad_step)
     finish(second)
-    far_terms(second, 1)
-    for d in range(reach - 2, 0, -1):
-        over_rest(d, value_step, second)
-        send_first(d, 1)
-    over_rest(0, value_step, second)
-    for d in range(reach - 1, 1, -1):
-        send_on(d, 1)
+    far_give(second, 1)
+    far_take(second, 1, 0)
     for d in range(reach - 1, 0, -1):
+
+        @pl.when((me >= d) & (me < reach))
+        def _():
+            rest_blocks(d, value_step, second)
+
+        if reach > 1:
+            send_on(d, 1, me >= max(d, 2))
         over_rest(d, grad_step, second)
         send_first(d, 0)
+        if d == reach - 1:
+            far_take(second, 1, 1)
+    over_rest(0, value_step, second)
     over_rest(0, grad_step, second)
     for i in range(second):
         finish(i)
-    far_terms(0, second)
+    far_give(0, second)
+    far_take(0, second, 0)
+    far_take(0, second, 1)
+    near_give()
     for d in range(reach - 1, 1, -1):
         send_on(d, 0)
-    near_terms()
+    near_take()
     if reach > 1:
-        send_on(1, 1)
-        send_on(1, 0, me == 1)
-    settle(1)
+        send_on(1, 1, me == 1)
+    settle(1, me >= 2)
     if reach > 1:
-        send_on(1, 0, me >= 2)
+        send_on(1, 0)
+    settle(1, me < 2)
 
     @pl.when(has_next)
     def _():
@@ -745,8 +824,12 @@
 
         @pl.when((me >= d) & has_next)
         def _():
-            for c in range(2):
-                forward(d, c).wait_send()
+            forward(d, 0).wait_send()
+            if d == reach - 1:
+                last_hop(0).wait_send()
+                last_hop(1).wait_send()
+            else:
+                forward(d, 1).wait_send()
 
         @pl.when(me >= d + 1)
         def _():
@@ -782,16 +865,16 @@
         ((rows, HEAD_WIDTH), half),
         ((rows, HEAD_WIDTH), half),
         ((rows, q_width), half),
-        ((rows, q_width), half),
-        ((rows, 2 * HEAD_WIDTH), half),
+        ((rows, q_width + 2 * HEAD_WIDTH), half),
+        ((pairs - 1, 2, q_width + 2 * HEAD_WIDTH, cols), half),
         ((2, rows, 2 * pairs * HEAD_WIDTH), half),
         ((2, cols, 2 * pairs * HEAD_WIDTH), half),
         (w_query.shape, half),
         (key_weight.shape, half),
         (value_weight.shape, half),
         ((rows, cols), full),
-        ((cols // math.gcd(cols, 256), rows, math.gcd(cols, 256)), half),
-        ((cols // math.gcd(cols, 256), rows, math.gcd(cols, 256)), half),
+        ((cols // math.gcd(cols, 512), rows, math.gcd(cols, 512)), half),
+        ((cols // math.gcd(cols, 512), rows, math.gcd(cols, 512)), half),
         ((pairs - 1, nb, 2, rows // nb, cols // 2), half),
         ((pairs - 1, nb, 2, rows // nb, cols // 2), half),
         ((pairs - 1, nb, 2, rows // nb, cols // 2), half),
@@ -821,8 +904,8 @@
         + [
             dma((5,)),
             dma((3,)),
-            dma((cols // math.gcd(cols, 256),)),
-            dma((cols // math.gcd(cols, 256),)),
+            dma((cols // math.gcd(cols, 512),)),
+            dma((cols // math.gcd(cols, 512),)),
             dma((pairs - 1, nb, 2)),
             dma((pairs - 1, nb, 2)),
             dma((pairs - 1, nb, 2)),
@@ -838,6 +921,8 @@
         + [
             dma((reach, 2)),
             dma((reach, 2)),
+            dma((2,)),
+            dma((2,)),
             dma((reach, 2)),
             dma((reach, 2)),
         ],

time: 54.1 us -> 51.7 us (0.956)
  the two profiles are of different devices: /device:TPU:9 before, /device:TPU:17 now
where the time goes in v4:
time: 51.7 us; the launch traced here: 51.6 us
  Pallas kernels  50.6 us (98%)
  local copies, waits for them, and re-layouts  0.97 us (2%)
    pallas_call x1, Pallas kernels, body(): pl.pallas_call(functools.partial(attention_kernel, shards, reach, places,...  50.6 us

profile of v4, /device:TPU:17, one launch (start us, length us, event | category | flops | bytes accessed | tf_op | source)
XLA Modules:
  0.0 51.6 jit_solution(8615619000817463678)
XLA Ops:
  0.0 50.6 %attention.1 = bf16[512,1024]{1,0:T(8,128)(2,1)S(1)} custom-call(bf16[512,512]{1,0:T(8,128)(2,1)} %q_hbm.1, bf16[512,128]{1,0:T(8,128)(2,1)} %k_hbm.1, bf16[512,128]{1,0:T(8,128)(2,1)} %v_hbm.1, bf16[512,512]{1,0:T(8,128)(2,1)} %g_hbm.1, s32[4,8]{1,0:T(4,128)} %docs_hbm.1, bf16[4096,512]{1,0:T(8,128)(2,1)} %wq_hbm.1, bf16[4096,128]{1,0:T(8,128)(2,1)} %wk_hbm.1, ...), custom_call_target="tpu_custom_call" | custom-call | tf_op jit(solution)/shard_map/attention/pallas_call | solution.py:897
  50.6 1.0 %copy.10 = bf16[512,1024]{1,0:T(8,128)(2,1)} copy(bf16[512,1024]{1,0:T(8,128)(2,1)S(1)} %attention.1) | data formatting | bytes 2097152

commit v5 on v4

--- a/solution.py
+++ b/solution.py
@@ -172,12 +172,14 @@
             device_id_type=MESH_ID,
         )
 
-    def backward(d, c):
+    spans = [slice(n * (rows // 2), (n + 1) * (rows // 2)) for n in range(2)]
+
+    def backward(d, c, n):
         return pltpu.make_async_remote_copy(
-            src_ref=ret_out.at[d - 1, c],
-            dst_ref=ret_in.at[d - 1, c],
-            send_sem=ret_send.at[d - 1, c],
-            recv_sem=ret_recv.at[d - 1, c],
+            src_ref=ret_out.at[d - 1, c, spans[n]],
+            dst_ref=ret_in.at[d - 1, c, spans[n]],
+            send_sem=ret_send.at[d - 1, c, n],
+            recv_sem=ret_recv.at[d - 1, c, n],
             device_id={"seq": jnp.maximum(me - 1, 0)},
             device_id_type=MESH_ID,
         )
@@ -228,7 +230,7 @@
     def _():
         forward(0, 0).start()
 
-        @pl.when(me != 1)
+        @pl.when((me != 1) | (parity == 0))
         def _():
             forward(0, 1).start()
 
@@ -389,23 +391,26 @@
         arrive(d, 1, False)
         over_blocks(d, step)
 
-    def scaled(d, c):
-        return kv_sum[d, c] * scale if c == 0 else kv_sum[d, c]
+    def scaled(d, c, n):
+        return kv_sum[d, c, spans[n]] * scale if c == 0 else kv_sum[d, c, spans[n]]
 
     def send_first(d, c, extra=True):
         first = me >= d if d == reach else (me >= d) & jnp.logical_not(has_next) & extra
 
         @pl.when(first)
         def _():
-            ret_out[d - 1, c] = scaled(d, c).astype(jnp.bfloat16)
-            backward(d, c).start()
+            for n in range(2):
+                ret_out[d - 1, c, spans[n]] = scaled(d, c, n).astype(jnp.bfloat16)
+                backward(d, c, n).start()
 
     def send_on(d, c, extra=None):
         @pl.when((me >= d if extra is None else extra) & has_next)
         def _():
-            backward(d + 1, c).wait_recv()
-            ret_out[d - 1, c] = (scaled(d, c) + ret_in[d, c].astype(jnp.float32)).astype(jnp.bfloat16)
-            backward(d, c).start()
+            for n in range(2):
+                backward(d + 1, c, n).wait_recv()
+                total = scaled(d, c, n) + ret_in[d, c, spans[n]].astype(jnp.float32)
+                ret_out[d - 1, c, spans[n]] = total.astype(jnp.bfloat16)
+                backward(d, c, n).start()
 
     present(0, score_step)
     present(0, delta_step)
@@ -426,12 +431,6 @@
 
     for d in range(1, reach + 1):
         arrive(d, 0)
-        if d == 1:
-
-            @pl.when((me == 1) & (parity == 0) & has_next)
-            def _():
-                forward(0, 1).start()
-
         present(d, score_step)
         if d == 1:
 
@@ -470,6 +469,11 @@
     def rest_blocks(d, step, count):
         if d in (0, reach):
             for i in range(count - 1, -1, -1):
+                step(d, i, False)
+            return
+
+        if reach <= 3 and count <= 2:
+            for i in range(count):
                 step(d, i, False)
             return
 
@@ -606,12 +610,12 @@
 
         both(step)
 
-    def gather(k, m, c):
+    def gather(k, m, c, n):
         return pltpu.make_async_remote_copy(
-            src_ref=dkv_all.at[c, :, slot(k, 0)] if m == 1 else dkv_all.at[c, :, slot(0, 0)],
-            dst_ref=dkv_all.at[c, :, slot(k, m)],
-            send_sem=gather_send.at[k, m, c],
-            recv_sem=gather_recv.at[k, m, c],
+            src_ref=dkv_all.at[c, spans[n], slot(k, 0)] if m == 1 else dkv_all.at[c, spans[n], slot(0, 0)],
+            dst_ref=dkv_all.at[c, spans[n], slot(k, m)],
+            send_sem=gather_send.at[k, m, c, n],
+            recv_sem=gather_recv.at[k, m, c, n],
             device_id={"tp": partner if m == 1 else peer_of(k)},
             device_id_type=MESH_ID,
         )
@@ -619,11 +623,14 @@
     def settle(c, extra=True):
         @pl.when(has_next & extra)
         def _():
-            backward(1, c).wait_recv()
-            dkv_all[c, :, 0:HEAD_WIDTH] = (scaled(0, c) + ret_in[0, c].astype(jnp.float32)).astype(jnp.bfloat16)
-            for k in range(1, pairs):
-                gather(k, 0, c).start()
-            gather(0, 1, c).start()
+            for n in range(2):
+                backward(1, c, n).wait_recv()
+                total = scaled(0, c, n) + ret_in[0, c, spans[n]].astype(jnp.float32)
+                dkv_all[c, spans[n], 0:HEAD_WIDTH] = total.astype(jnp.bfloat16)
+                for k in range(1, pairs):
+                    gather(k, 0, c, n).start()
+            for n in range(2):
+                gather(0, 1, c, n).start()
 
     def add_terms(k, c):
         lanes = slice(2 * k * HEAD_WIDTH, (2 * k + 2) * HEAD_WIDTH)
@@ -632,17 +639,20 @@
             near_sum[:, n : n + step_cols] += dot_t(dkv_all[c, :, lanes], kw_all[c, n : n + step_cols, lanes])
 
     def near_adds(c):
-        gather(0, 1, c).wait_recv()
+        for n in range(2):
+            gather(0, 1, c, n).wait_recv()
         add_terms(0, c)
 
     def far_passes(c):
         for k in range(1, pairs):
-            gather(k, 0, c).wait_recv()
-            gather(k, 1, c).start()
+            for n in range(2):
+                gather(k, 0, c, n).wait_recv()
+                gather(k, 1, c, n).start()
 
     def far_adds(c):
         for k in range(1, pairs):
-            gather(k, 1, c).wait_recv()
+            for n in range(2):
+                gather(k, 1, c, n).wait_recv()
             add_terms(k, c)
 
     present(reach, value_step)
@@ -650,13 +660,13 @@
     over_near(top, value_step)
 
 
-    for d in range(reach - 1, 0, -1):
+    if reach > 1:
 
         @pl.when(me >= reach)
         def _():
-            rest_blocks(d, value_step, top)
-
-        send_first(d, 1)
+            rest_blocks(reach - 1, value_step, top)
+
+        send_first(reach - 1, 1, me >= reach)
 
     def late_deltas(step):
         for d in range(1, reach):
@@ -690,8 +700,8 @@
         grad_step(reach, top, False)
 
     finish(top)
+    far_take(top, 1, 0)
     far_give(top, 1)
-    far_take(top, 1, 0)
 
     if relayed:
 
@@ -716,7 +726,7 @@
             value_step(d, i, fresh)
         else:
 
-            @pl.when(me < reach)
+            @pl.when((d < reach - 1) | (me < reach))
             def _():
                 value_step(d, i, fresh)
 
@@ -729,14 +739,16 @@
     over_near(second, second_value)
     over_near(second, grad_step)
     finish(second)
+    far_take(second, 1, 0)
     far_give(second, 1)
-    far_take(second, 1, 0)
     for d in range(reach - 1, 0, -1):
 
-        @pl.when((me >= d) & (me < reach))
+        @pl.when(me == d if d == reach - 1 else me >= d)
         def _():
             rest_blocks(d, value_step, second)
 
+        if d < reach - 1:
+            send_first(d, 1)
         if reach > 1:
             send_on(d, 1, me >= max(d, 2))
         over_rest(d, grad_step, second)
@@ -747,8 +759,8 @@
     over_rest(0, grad_step, second)
     for i in range(second):
         finish(i)
+    far_take(0, second, 0)
     far_give(0, second)
-    far_take(0, second, 0)
     far_take(0, second, 1)
     near_give()
     for d in range(reach - 1, 1, -1):
@@ -756,10 +768,9 @@
     near_take()
     if reach > 1:
         send_on(1, 1, me == 1)
-    settle(1, me >= 2)
     if reach > 1:
         send_on(1, 0)
-    settle(1, me < 2)
+    settle(1)
 
     @pl.when(has_next)
     def _():
@@ -804,7 +815,8 @@
     def _():
         for k, m in others:
             for c in range(2):
-                gather(k, m, c).wait_send()
+                for n in range(2):
+                    gather(k, m, c, n).wait_send()
         for item in fetches:
             fetch(*item).wait_send()
         if relayed:
@@ -834,7 +846,8 @@
         @pl.when(me >= d + 1)
         def _():
             for c in range(2):
-                backward(d + 1, c).wait_send()
+                for n in range(2):
+                    backward(d + 1, c, n).wait_send()
 
 
 def body(
@@ -914,8 +927,8 @@
             dma((pairs, 2, 2)),
             dma((pairs, 2)),
             dma((pairs, 2)),
-            dma((pairs, 2, 2)),
-            dma((pairs, 2, 2)),
+            dma((pairs, 2, 2, 2)),
+            dma((pairs, 2, 2, 2)),
         ]
         + [pltpu.VMEM(*item) for item in later]
         + [
@@ -923,8 +936,8 @@
             dma((reach, 2)),
             dma((2,)),
             dma((2,)),
-            dma((reach, 2)),
-            dma((reach, 2)),
+            dma((reach, 2, 2)),
+            dma((reach, 2, 2)),
         ],
         compiler_params=pltpu.CompilerParams(
             collective_id=0, has_side_effects=True, vmem_limit_bytes=limit

time: 51.7 us -> 51.1 us (0.988)
  Pallas kernels: 50.6 us -> 49.9 us
    pallas_call x1, Pallas kernels: 50.6 us -> 49.9 us  [body(): pl.pallas_call(functools.partial(attention_kernel, shards, reach, places,...]
where the time goes in v5:
time: 51.1 us; the launch traced here: 50.9 us
  Pallas kernels  49.9 us (98%)
  local copies, waits for them, and re-layouts  0.97 us (2%)
    pallas_call x1, Pallas kernels, body(): pl.pallas_call(functools.partial(attention_kernel, shards, reach, places,...  49.9 us

profile of v5, /device:TPU:17, one launch (start us, length us, event | category | flops | bytes accessed | tf_op | source)
XLA Modules:
  0.0 50.9 jit_solution(6453344156064438990)
XLA Ops:
  0.0 49.9 %attention.1 = bf16[512,1024]{1,0:T(8,128)(2,1)S(1)} custom-call(bf16[512,512]{1,0:T(8,128)(2,1)} %q_hbm.1, bf16[512,128]{1,0:T(8,128)(2,1)} %k_hbm.1, bf16[512,128]{1,0:T(8,128)(2,1)} %v_hbm.1, bf16[512,512]{1,0:T(8,128)(2,1)} %g_hbm.1, s32[4,8]{1,0:T(4,128)} %docs_hbm.1, bf16[4096,512]{1,0:T(8,128)(2,1)} %wq_hbm.1, bf16[4096,128]{1,0:T(8,128)(2,1)} %wk_hbm.1, ...), custom_call_target="tpu_custom_call" | custom-call | tf_op jit(solution)/shard_map/attention/pallas_call | solution.py:910
  49.9 1.0 %copy.10 = bf16[512,1024]{1,0:T(8,128)(2,1)} copy(bf16[512,1024]{1,0:T(8,128)(2,1)S(1)} %attention.1) | data formatting | bytes 2097152

commit v6 on v5

--- a/solution.py
+++ b/solution.py
@@ -759,8 +759,8 @@
     over_rest(0, grad_step, second)
     for i in range(second):
         finish(i)
+    far_give(0, second)
     far_take(0, second, 0)
-    far_give(0, second)
     far_take(0, second, 1)
     near_give()
     for d in range(reach - 1, 1, -1):

time: 51.1 us -> 51.3 us (level)
  no operation moved by 1% of the time
where the time goes in v6:
time: 51.3 us; the launch traced here: 51.2 us
  Pallas kernels  50.2 us (98%)
  local copies, waits for them, and re-layouts  0.97 us (2%)
    pallas_call x1, Pallas kernels, body(): pl.pallas_call(functools.partial(attention_kernel, shards, reach, places,...  50.2 us

profile of v6, /device:TPU:17, one launch (start us, length us, event | category | flops | bytes accessed | tf_op | source)
XLA Modules:
  0.0 51.2 jit_solution(12260326454930272927)
XLA Ops:
  0.0 50.2 %attention.1 = bf16[512,1024]{1,0:T(8,128)(2,1)S(1)} custom-call(bf16[512,512]{1,0:T(8,128)(2,1)} %q_hbm.1, bf16[512,128]{1,0:T(8,128)(2,1)} %k_hbm.1, bf16[512,128]{1,0:T(8,128)(2,1)} %v_hbm.1, bf16[512,512]{1,0:T(8,128)(2,1)} %g_hbm.1, s32[4,8]{1,0:T(4,128)} %docs_hbm.1, bf16[4096,512]{1,0:T(8,128)(2,1)} %wq_hbm.1, bf16[4096,128]{1,0:T(8,128)(2,1)} %wk_hbm.1, ...), custom_call_target="tpu_custom_call" | custom-call | tf_op jit(solution)/shard_map/attention/pallas_call | solution.py:910
  50.2 1.0 %copy.10 = bf16[512,1024]{1,0:T(8,128)(2,1)} copy(bf16[512,1024]{1,0:T(8,128)(2,1)S(1)} %attention.1) | data formatting | bytes 2097152
